TPU v7x, 512 devices: a whole 4x4x16 slice. The times are simulated.
512 devices in a mesh: leaf: 32 (over z, core), region: 16 (over x, y).
Axes of the slice: x: 4, y: 4, z: 16, core: 2. Of those that a mesh axis runs over, the one named last changes fastest.
Arguments:
- leaf_factor: bfloat16 [16, 32768, 1024], P('region', 'leaf'), as said below
- basis_pool: bfloat16 [16, 32768, 512], P('region', 'leaf'), may hold values from -6 to 6
- root_basis: bfloat16 [16, 32768, 256], P('region', 'leaf'), may hold values from -6 to 6
- responses: bfloat16 [16, 32768, 256], P('region', 'leaf'), may hold values from -48 to 48
- knot_order: int32 [16, 512], P('region'), may hold values from 0 to 511, each once within a row
- region_prior: bfloat16 [16, 256, 256], P('region'), as said below
- root_prior: bfloat16 [256, 256], replicated, as said below
Outputs:
- predictions: bfloat16 [16, 32768, 256], P('region', 'leaf')
- region_factor: float32 [16, 256, 256], P('region', 'leaf')
- root_factor: float32 [256, 256], P('leaf')
Inputs may be any that keep to these rules, and one draw needn't show every extreme that they name: `knot_order`: each row lists every candidate column exactly once. `leaf_factor`: each leaf block has a diagonal near one that dominates its other entries. `region_prior`: symmetric and positive definite. `root_prior`: symmetric and positive definite.
All inputs are finite; a program needn't handle non-finite values.
Results may differ from a plain program's by a relative error of at most 0.0038.
Values sent between devices are 32-bit elements; how exact they have to be, the bound alone decides.
No kernel may reach another device: no remote copies, remote signals or barrier semaphores. Data moves between devices by JAX's collectives and lax.ppermute only.
A program may use at most 64 MiB of HBM per device.

v0:
```python
import math

import jax
import jax.numpy as jnp
from jax import lax
from jax.sharding import PartitionSpec as P


def padded_to(lines, size):
    spare = -lines.shape[0] % size
    if not spare:
        return lines
    return jnp.concatenate([lines, jnp.zeros((spare, *lines.shape[1:]), lines.dtype)])


def sent_to_all(shard, axis):
    size = lax.axis_size(axis)
    return lax.all_to_all(
        jnp.broadcast_to(shard[None], (size, *shard.shape)), axis, 0, 0, tiled=True
    )


def laid_out(tiles, dim):
    tiles = jnp.moveaxis(tiles, 0, dim)
    lengths = tiles.shape
    return tiles.reshape(*lengths[:dim], lengths[dim] * lengths[dim + 1], *lengths[dim + 2 :])


def gathered_copies(shard, axis, dim):
    tiles = sent_to_all(shard, axis)
    return laid_out(tiles, dim)


def split_up(shard, dim, size):
    before, after = (shard.shape[:dim], shard.shape[dim + 1 :])
    return jnp.moveaxis(shard.reshape(*before, size, -1, *after), dim, 0)


def sum_at_owner(shard, axis, dim):
    tiles = split_up(shard, dim, lax.axis_size(axis))
    arrived = lax.all_to_all(tiles, axis, split_axis=0, concat_axis=0, tiled=True)
    return arrived.sum(axis=0)


def nested_sum(shard, axes):
    padded = padded_to(shard, lax.axis_size(axes))
    whole = gathered_copies(sum_at_owner(padded, axes, 0), axes, 0)
    return lax.slice_in_dim(whole, 0, len(shard)).reshape(shard.shape)


def in_one(arrays, axis):
    flat, at, done = (jnp.concatenate([a.reshape(-1) for a in arrays]), 0, [])
    total = nested_sum(flat, axis)
    for a in arrays:
        done.append(total[at : at + a.size].reshape(a.shape))
        at += a.size
    return tuple(done)


def sum_by_parts(shard, axes):
    lines = shard.reshape(-1, shard.shape[-1])
    own = sum_at_owner(padded_to(lines, lax.axis_size(axes)), axes, 0)
    whole = gathered_copies(own, axes, 0)
    return whole[: len(lines)].reshape(shard.shape)


def contract_rows(left, right):
    return lax.dot_general(
        left, right, (((0,), (0,)), ((), ())), preferred_element_type=jnp.float32
    )


def per_device(
    leaf_factor, basis_pool, root_basis, responses, knot_order, region_prior, root_prior
):
    knot_count = region_prior.shape[1]
    root_count = root_prior.shape[0]
    num_leaf = lax.axis_size("leaf")
    num_region = lax.axis_size("region")
    leaf_rows = leaf_factor.shape[2]
    knot_ids = knot_order[0, :knot_count]
    region_basis = jnp.take(basis_pool[0], knot_ids, axis=1)
    root_cols = root_basis[0]
    joined = jnp.concatenate([region_basis, root_cols, responses[0]], axis=1)
    white = contract_rows(leaf_factor[0], joined).astype(jnp.bfloat16)
    gram_b = contract_rows(white[:, :knot_count], white)
    gram_a = contract_rows(white[:, knot_count : knot_count + root_count], white[:, knot_count:])
    prior_mat = region_prior[0].astype(jnp.float32)
    region_part, root_part = in_one((gram_b, gram_a), "leaf")
    system = prior_mat + region_part[:, :knot_count]
    chol_region = jnp.linalg.cholesky(system)
    solved = jax.scipy.linalg.cho_solve((chol_region, True), region_part[:, knot_count:])
    reduced = jnp.dot(
        region_part[:, knot_count : knot_count + root_count].T,
        solved,
        precision=lax.Precision.HIGHEST,
    )
    chol_region, solved, reduced = (chol_region, solved, reduced)
    summed = sum_by_parts(root_part - reduced, "region")
    schur_mat = root_prior.astype(jnp.float32) + summed[:, :root_count]
    chol_root = jnp.linalg.cholesky(schur_mat)
    root_coef = jax.scipy.linalg.cho_solve((chol_root, True), summed[:, root_count:])
    region_coef = solved[:, root_count:] - jnp.dot(
        solved[:, :root_count], root_coef, precision=lax.Precision.HIGHEST
    )
    mean_out = jnp.dot(
        region_basis, region_coef.astype(jnp.bfloat16), preferred_element_type=jnp.float32
    )
    mean_out = mean_out + jnp.dot(
        root_cols, root_coef.astype(jnp.bfloat16), preferred_element_type=jnp.float32
    )
    predictions = mean_out.astype(jnp.bfloat16)[None]
    obs_region = leaf_rows * num_leaf
    leaf_pos = lax.axis_index("leaf")
    knot_rows = knot_count // num_leaf
    root_rows = root_count // num_leaf
    region_slice = lax.dynamic_slice_in_dim(chol_region, leaf_pos * knot_rows, knot_rows, 0)
    root_slice = lax.dynamic_slice_in_dim(chol_root, leaf_pos * root_rows, root_rows, 0)
    region_factor = (region_slice / math.sqrt(obs_region))[None]
    root_factor = root_slice / math.sqrt(obs_region * num_region)
    return (predictions, region_factor, root_factor)


def solution(mesh):
    placed = (
        P("region", "leaf", None),
        P("region", "leaf", None),
        P("region", "leaf", None),
        P("region", "leaf", None),
        P("region", None),
        P("region", None, None),
        P(),
    )
    return jax.shard_map(
        per_device,
        mesh=mesh,
        in_specs=placed,
        out_specs=(P("region", "leaf", None), P("region", "leaf", None), P("leaf", None)),
        check_vma=False,
    )
```

profile of v0, /device:TPU:8, one launch (start us, length us, event | category | flops | bytes accessed | tf_op | source)
XLA Modules:
  0.0 378.0 jit_solution(4924458375958087776)
XLA Ops:
  5.1 2.0 copy.51
  10.2 3.0 fusion.2
  17.7 15.5 %all-to-all-start = ((f32[32,1,10240]{2,1,0:T(1,128)}), f32[32,1,10240]{2,1,0:T(1,128)S(1)}, u32[]{:S(2)}, u32[]{:S(2)}) async-start(f32[32,1,10240]{2,1,0:T(1,128)} %bitcast.116), calls=%async_computation | async-start | bytes 2621440 | tf_op jit(solution)/shard_map/all_to_all | solution.py:41
  33.2 67.1 %all-to-all-done = f32[32,1,10240]{2,1,0:T(1,128)S(1)} async-done(((f32[32,1,10240]{2,1,0:T(1,128)}), f32[32,1,10240]{2,1,0:T(1,128)S(1)}, u32[]{:S(2)}, u32[]{:S(2)}) %all-to-all-start) | async-done | bytes 1310752 | tf_op jit(solution)/shard_map/all_to_all | solution.py:41
  102.8 4.1 %all-to-all-start.1 = ((f32[32,1,10240]{2,1,0:T(1,128)}), f32[32,1,10240]{2,1,0:T(1,128)S(1)}, u32[]{:S(2)}, u32[]{:S(2)}) async-start(f32[32,1,10240]{2,1,0:T(1,128)} %broadcast_in_dim.31), calls=%async_computation.1 | async-start | bytes 2621440 | tf_op jit(solution)/shard_map/all_to_all | solution.py:18
  107.9 66.7 %all-to-all-done.1 = f32[32,1,10240]{2,1,0:T(1,128)S(1)} async-done(((f32[32,1,10240]{2,1,0:T(1,128)}), f32[32,1,10240]{2,1,0:T(1,128)S(1)}, u32[]{:S(2)}, u32[]{:S(2)}) %all-to-all-start.1) | async-done | bytes 1310752 | tf_op jit(solution)/shard_map/all_to_all | solution.py:18
  175.6 2.2 reshape.113
  186.4 11.7 %cholesky.130 = f32[128,128]{1,0:T(8,128)S(1)} custom-call(f32[128,128]{1,0:T(8,128)S(1)} %cholesky.194), custom_call_target="Cholesky" | custom-call | tf_op jit(solution)/shard_map/jit(cholesky)/cholesky | solution.py:91
  198.1 10.4 %custom-call.25 = f32[1,128,128]{1,2,0:T(8,128)} custom-call(f32[1,128,128]{2,1,0:T(8,128)S(1)} %get-tuple-element.51), custom_call_target="InvertDiagBlocksLowerTriangular" | custom-call | tf_op jit(solution)/shard_map/jit(cholesky)/cholesky | solution.py:91
  212.1 11.7 %cholesky.147 = f32[128,128]{1,0:T(8,128)S(1)} custom-call(f32[128,128]{1,0:T(8,128)S(1)} %convolution_subtract_fusion.7), custom_call_target="Cholesky" | custom-call | tf_op jit(solution)/shard_map/jit(cholesky)/cholesky | solution.py:91
  228.3 5.8 %while.2 = (s32[]{:T(128)}, f32[256,256]{1,0:T(8,128)}, s32[2,2]{1,0:T(2,128)S(1)}, f32[2,128,128]{2,1,0:T(8,128)S(1)}, s32[]{:T(128)}) while((s32[]{:T(128)}, f32[256,256]{1,0:T(8,128)}, s32[2,2]{1,0:T(2,128)S(1)}, f32[2,128,128]{2,1,0:T(8,128)S(1)}, s32[]{:T(128)}) %tuple.47), condition=%wide.while_cond, body=%wide.while_body.sunk | while | flops 2 | bytes 131181 | solution.py:92
  229.0 2.2 bitcast_dynamic-update-slice_fusion.4
  231.9 2.2 bitcast_dynamic-update-slice_fusion.4
  234.8 20.7 %custom-call.22 = f32[2,128,128]{1,2,0:T(8,128)S(1)} custom-call(f32[2,128,128]{2,1,0:T(8,128)} %copy-done.10), custom_call_target="InvertDiagBlocksLowerTriangular" | custom-call | tf_op jit(solution)/shard_map/jit(_cho_solve)/triangular_solve | solution.py:92
  262.0 4.5 %reduce.9 = f32[32,10240]{1,0:T(8,128)} reduce(f32[32,1,10240]{2,1,0:T(1,128)S(1)} %all-to-all-done.1, f32[]{:T(128)} %constant.158), dimensions={1}, to_apply=%all_to_all.18.reduce_sub_computation | reduce | bytes 2621444 | tf_op jit(solution)/shard_map/all_to_all | solution.py:18
  266.5 2.8 slice.133
  271.1 16.8 %all_to_all.25 = f32[16,16,512]{2,1,0:T(8,128)S(1)} all-to-all(f32[16,16,512]{2,1,0:T(8,128)S(1)} %bitcast.120), channel_id=1, replica_groups=mesh['leaf'=32,'region'=16] {'region'}, dimensions={0} | all-to-all | bytes 1048576 | tf_op jit(solution)/shard_map/all_to_all | solution.py:41
  288.8 5.2 %all-to-all-start.3 = ((f32[16,16,512]{2,1,0:T(8,128)}), f32[16,16,512]{2,1,0:T(8,128)S(1)}, u32[]{:S(2)}, u32[]{:S(2)}) async-start(f32[16,16,512]{2,1,0:T(8,128)} %broadcast_in_dim.32), calls=%async_computation.3 | async-start | bytes 1048576 | tf_op jit(solution)/shard_map/all_to_all | solution.py:18
  296.3 6.4 %all-to-all-done.3 = f32[16,16,512]{2,1,0:T(8,128)S(1)} async-done(((f32[16,16,512]{2,1,0:T(8,128)}), f32[16,16,512]{2,1,0:T(8,128)S(1)}, u32[]{:S(2)}, u32[]{:S(2)}) %all-to-all-start.3) | async-done | bytes 524320 | tf_op jit(solution)/shard_map/all_to_all | solution.py:18
  307.1 11.7 %cholesky.164 = f32[128,128]{1,0:T(8,128)S(1)} custom-call(f32[128,128]{1,0:T(8,128)S(1)} %cholesky.197), custom_call_target="Cholesky" | custom-call | tf_op jit(solution)/shard_map/jit(cholesky)/cholesky | solution.py:101
  318.9 9.8 %custom-call.26 = f32[1,128,128]{1,2,0:T(8,128)S(1)} custom-call(f32[1,128,128]{2,1,0:T(8,128)S(1)} %get-tuple-element.47), custom_call_target="InvertDiagBlocksLowerTriangular" | custom-call | tf_op jit(solution)/shard_map/jit(cholesky)/cholesky | solution.py:101
  330.8 11.7 %cholesky.181 = f32[128,128]{1,0:T(8,128)S(1)} custom-call(f32[128,128]{1,0:T(8,128)S(1)} %convolution_subtract_fusion.6), custom_call_target="Cholesky" | custom-call | tf_op jit(solution)/shard_map/jit(cholesky)/cholesky | solution.py:101
  346.9 4.0 %while.3 = (s32[]{:T(128)}, f32[256,256]{1,0:T(8,128)S(1)}, s32[2,2]{1,0:T(2,128)S(1)}, f32[2,128,128]{2,1,0:T(8,128)S(1)}, s32[]{:T(128)}) while((s32[]{:T(128)}, f32[256,256]{1,0:T(8,128)S(1)}, s32[2,2]{1,0:T(2,128)S(1)}, f32[2,128,128]{2,1,0:T(8,128)S(1)}, s32[]{:T(128)}) %tuple.53), condition=%wide.while_cond.1, body=%wide.while_body.1.sunk | while | flops 2 | bytes 131181 | solution.py:102
  351.5 20.8 %custom-call.23 = f32[2,128,128]{1,2,0:T(8,128)S(1)} custom-call(f32[2,128,128]{2,1,0:T(8,128)} %copy-done.9), custom_call_target="InvertDiagBlocksLowerTriangular" | custom-call | tf_op jit(solution)/shard_map/jit(_cho_solve)/triangular_solve | solution.py:102
  (102 shorter events, 64.6 us)
Async XLA Ops:
  0.6 9.6 %copy-start = (bf16[1,1024,1024]{2,1,0:T(8,128)(2,1)S(1)}, bf16[1,1024,1024]{2,1,0:T(8,128)(2,1)}, u32[]{:S(2)}) copy-start(bf16[1,1024,1024]{2,1,0:T(8,128)(2,1)} %param.8) | copy-start | bytes 6291460
  0.6 2.3 slice-start
  17.7 82.6 %all-to-all-start = ((f32[32,1,10240]{2,1,0:T(1,128)}), f32[32,1,10240]{2,1,0:T(1,128)S(1)}, u32[]{:S(2)}, u32[]{:S(2)}) async-start(f32[32,1,10240]{2,1,0:T(1,128)} %bitcast.116), calls=%async_computation | async-start | bytes 2621440 | tf_op jit(solution)/shard_map/all_to_all | solution.py:41
  102.8 71.8 %all-to-all-start.1 = ((f32[32,1,10240]{2,1,0:T(1,128)}), f32[32,1,10240]{2,1,0:T(1,128)S(1)}, u32[]{:S(2)}, u32[]{:S(2)}) async-start(f32[32,1,10240]{2,1,0:T(1,128)} %broadcast_in_dim.31), calls=%async_computation.1 | async-start | bytes 2621440 | tf_op jit(solution)/shard_map/all_to_all | solution.py:18
  185.7 0.7 copy-start.7
  234.1 0.6 copy-start.10
  259.0 0.7 copy-start.1
  266.5 2.8 copy-start.2
  266.5 2.8 copy-start.4
  288.8 13.9 %all-to-all-start.3 = ((f32[16,16,512]{2,1,0:T(8,128)}), f32[16,16,512]{2,1,0:T(8,128)S(1)}, u32[]{:S(2)}, u32[]{:S(2)}) async-start(f32[16,16,512]{2,1,0:T(8,128)} %broadcast_in_dim.32), calls=%async_computation.3 | async-start | bytes 1048576 | tf_op jit(solution)/shard_map/all_to_all | solution.py:18
  306.4 0.7 copy-start.8
  342.6 2.6 copy-start.6
  350.8 0.7 copy-start.9
  372.6 1.9 copy-start.3
  374.0 1.0 copy-start.5
where the time goes:
time: 385 us; the launch traced here: 378 us
  waiting for transfers between devices  140 us (36%)
  other arithmetic  131 us (34%)
  local copies, waits for them, and re-layouts  40.3 us (10%)
  starting transfers between devices  24.8 us (6%)
  matrix products  21.2 us (6%)
  blocking collectives  16.8 us (4%)
  between operations  4.07 us (1%)
    all_to_all x2, waiting for transfers between devices, sent_to_all(): lax.all_to_all(jnp.broadcast_to(shard[None], (size, *shard.shape)), axis,...  73.1 us
    all_to_all x1, waiting for transfers between devices, sum_at_owner(): lax.all_to_all(tiles, axis, split_axis=0, concat_axis=0, tiled=True)  67.1 us
    another operation x6, other arithmetic, per_device(): chol_region = jnp.linalg.cholesky(system)  35.3 us
    another operation x7, other arithmetic, per_device(): chol_root = jnp.linalg.cholesky(schur_mat)  34.6 us
    another operation x3, other arithmetic, per_device(): jax.scipy.linalg.cho_solve((chol_region, True), region_part[:, knot_count:])  22.5 us
    another operation x2, other arithmetic, per_device(): jax.scipy.linalg.cho_solve((chol_root, True), summed[:, root_count:])  22.4 us
    all_to_all x1, blocking collectives, sum_at_owner(): lax.all_to_all(tiles, axis, split_axis=0, concat_axis=0, tiled=True)  16.8 us
    all_to_all x1, starting transfers between devices, sum_at_owner(): lax.all_to_all(tiles, axis, split_axis=0, concat_axis=0, tiled=True)  15.5 us
  transfers between devices with their start and end apart: 3, of which 3 were waited for; matrix products, arithmetic and copies ran while one was open for 1% of the time, Pallas kernels for 0%

commit v1 on v0

v1 whole, which is shorter than its diff:
```python
import math

import jax
import jax.numpy as jnp
from jax import lax
from jax.experimental import pallas as pl
from jax.experimental.pallas import tpu as pltpu
from jax.sharding import PartitionSpec as P

STEP = 16
HI = lax.Precision.HIGHEST
F32 = jnp.float32
BF16 = jnp.bfloat16


def rows_dot(left, right, precision=None):
    return lax.dot_general(
        left, right, (((0,), (0,)), ((), ())), precision=precision, preferred_element_type=F32
    )


def one_hot(knots, pool):
    count = knots.shape[1]
    ids = lax.broadcasted_iota(jnp.int32, (pool, count), 0)
    return (ids == knots).astype(BF16)


def grams_kernel(core_ref, knot_ref, factor_ref, pool_ref, root_ref, resp_ref,
                 keep_ref, send_ref, joined, total):
    step = pl.program_id(0)
    knots = total.shape[2] * total.shape[0] * total.shape[1]
    roots = root_ref.shape[2]

    @pl.when(step == 0)
    def _():
        pick = one_hot(knot_ref[:, :knots], pool_ref.shape[2])
        basis = jnp.dot(pool_ref[0], pick, preferred_element_type=F32)
        joined[:, :knots] = basis.astype(BF16)
        joined[:, knots : knots + roots] = root_ref[0]
        joined[:, knots + roots :] = resp_ref[0]
        total[...] = jnp.zeros_like(total)

    white = rows_dot(factor_ref[0], joined[...]).astype(BF16)
    gram_b = rows_dot(white[:, :knots], white)
    gram_a = rows_dot(white[:, knots : knots + roots], white[:, knots:])
    width = gram_b.shape[1]
    total[:, :, :, :width] += gram_b.reshape(*total.shape[:3], width)
    total[:, :, :, width:] += gram_a.reshape(*total.shape[:3], gram_a.shape[1])

    @pl.when(step == pl.num_programs(0) - 1)
    def _():
        core = core_ref[0]
        keep_ref[...] = total[:, core]
        send_ref[...] = total[:, 1 - core]


def split3(x):
    high = x.astype(BF16)
    rest = x - high.astype(F32)
    mid = rest.astype(BF16)
    low = (rest - mid.astype(F32)).astype(BF16)
    return high, mid, low


def factor_inverse(work, diag, panel):
    size = work.shape[0]

    def block(k, _):
        start = pl.multiple_of(k * STEP, STEP)
        tile = pl.multiple_of((start // 128) * 128, 128)
        corner = work[pl.ds(start, STEP), pl.ds(tile, 128)]
        diag[...] = pltpu.roll(corner, lax.rem(128 - (start - tile), 128), 1)
        lane = lax.broadcasted_iota(jnp.int32, (8, size), 1)
        inside = (lane >= start) & (lane < start + STEP)
        d, v = [], []
        for i in range(STEP):
            row = jnp.broadcast_to(diag[i : i + 1, :], (8, 128))
            d.append([None] * i + [jnp.broadcast_to(row[:, j : j + 1], (8, 128)) for j in range(i, STEP)])
            full = jnp.broadcast_to(work[pl.ds(start + i, 1), :], (8, size))
            v.append(jnp.where(inside, jnp.where(lane == start + i, 1.0, 0.0), full))
        for p in range(STEP):
            scale = lax.rsqrt(d[p][p])
            u = [None] * (p + 1) + [d[p][j] * scale for j in range(p + 1, STEP)]
            wide = jnp.concatenate([scale] * (size // 128), axis=1)
            done = v[p] * wide
            panel[p : p + 1, :] = done[0:1, :]
            for i in range(p + 1, STEP):
                for j in range(i, STEP):
                    d[i][j] = d[i][j] - u[i] * u[j]
                v[i] = v[i] - jnp.concatenate([u[i]] * (size // 128), axis=1) * done
        rows = panel[...]
        lane_p = lax.broadcasted_iota(jnp.int32, (STEP, size), 1)
        high, mid, low = split3(rows)
        later = lane_p >= start + STEP
        zero = jnp.zeros_like(high)
        th, tm, tl = (jnp.where(later, x, zero) for x in (high, mid, low))
        left = jnp.concatenate([th, th, tm, th, tl, tm], axis=0)
        right = jnp.concatenate([high, mid, high, low, high, mid], axis=0)
        change = rows_dot(left, right)
        lane_a = lax.broadcasted_iota(jnp.int32, (size, size), 1)
        row_a = lax.broadcasted_iota(jnp.int32, (size, size), 0)
        fresh = (lane_a >= start) & (lane_a < start + STEP) & (row_a >= start + STEP)
        work[...] = jnp.where(fresh, 0.0, work[...]) - change
        work[pl.ds(start, STEP), :] = rows
        return 0

    lax.fori_loop(0, size // STEP, block, 0)
    lane = lax.broadcasted_iota(jnp.int32, (size, size), 1)
    row = lax.broadcasted_iota(jnp.int32, (size, size), 0)
    return jnp.where(lane <= row, work[...], 0.0)


def factor_rows(matrix, first, inverse, scale):
    count = 8
    part = matrix[pl.ds(pl.multiple_of(first, 8), count), :]
    rows = lax.dot_general(
        part, inverse, (((1,), (1,)), ((), ())), precision=HI, preferred_element_type=F32
    )
    lane = lax.broadcasted_iota(jnp.int32, rows.shape, 1)
    row = lax.broadcasted_iota(jnp.int32, rows.shape, 0) + first
    return jnp.where(lane <= row, rows, 0.0) * scale


def region_kernel(scale, leaf_ref, gathered_ref, prior_ref, own_ref,
                  solved_ref, schur_ref, factor_ref, matrix, work, diag, panel, full):
    size = matrix.shape[0]
    first = leaf_ref[0] * 8
    matrix[...] = prior_ref[0].astype(F32) + gathered_ref[:, :size]
    work[...] = matrix[...]
    inverse = factor_inverse(work, diag, panel)
    half = jnp.dot(inverse, gathered_ref[:, size:], precision=HI, preferred_element_type=F32)
    roots = full.shape[0]
    full[...] = rows_dot(half[:, :roots], half, HI)
    schur_ref[...] = own_ref[...] - full[pl.ds(pl.multiple_of(first, 8), 8), :]
    solved_ref[...] = rows_dot(inverse, half, HI)
    factor_ref[0] = factor_rows(matrix, first, inverse, scale)


def root_kernel(scale, leaf_ref, summed_ref, prior_ref, solved_ref, knot_ref, pool_hbm, root_hbm,
                pred_ref, factor_ref, matrix, work, diag, panel, pool, root, sems):
    size = matrix.shape[0]
    loads = [
        pltpu.make_async_copy(pool_hbm.at[0], pool, sems.at[0]),
        pltpu.make_async_copy(root_hbm.at[0], root, sems.at[1]),
    ]
    for load in loads:
        load.start()
    first = leaf_ref[0] * 8
    matrix[...] = prior_ref[...].astype(F32) + summed_ref[:, :size]
    work[...] = matrix[...]
    inverse = factor_inverse(work, diag, panel)
    half = jnp.dot(inverse, summed_ref[:, size:], precision=HI, preferred_element_type=F32)
    root_coef = rows_dot(inverse, half, HI)
    coef = solved_ref[:, size:] - jnp.dot(
        solved_ref[:, :size], root_coef, precision=HI, preferred_element_type=F32
    )
    knots = coef.shape[0]
    pick = one_hot(knot_ref[:, :knots], pool.shape[1])
    spread = jnp.dot(pick, coef.astype(BF16), preferred_element_type=F32).astype(BF16)
    factor_ref[...] = factor_rows(matrix, first, inverse, scale)
    for load in loads:
        load.wait()
    mean = jnp.dot(pool[...], spread, preferred_element_type=F32)
    mean = mean + jnp.dot(root[...], root_coef.astype(BF16), preferred_element_type=F32)
    pred_ref[0] = mean.astype(BF16)


VMEM = pl.BlockSpec(memory_space=pltpu.VMEM)
SMEM = pl.BlockSpec(memory_space=pltpu.SMEM)
ANY = pl.BlockSpec(memory_space=pl.ANY)


def per_device(
    leaf_factor, basis_pool, root_basis, responses, knot_order, region_prior, root_prior
):
    knots = region_prior.shape[1]
    roots = root_prior.shape[0]
    cols = responses.shape[2]
    leaf_count = lax.axis_size("leaf")
    region_count = lax.axis_size("region")
    chips = leaf_count // 2
    rows = leaf_factor.shape[2]
    pool = basis_pool.shape[2]
    leaf = lax.axis_index("leaf").astype(jnp.int32)
    leaf_at = leaf.reshape(1)
    core_at = lax.rem(leaf, 2).reshape(1)
    share = knots // leaf_count
    wide_b = knots + roots + cols
    wide_a = roots + cols
    block = rows // 4

    def fixed(shape):
        return pl.BlockSpec(shape, lambda i: (0,) * len(shape))

    piece = jax.ShapeDtypeStruct((chips, share, wide_b + wide_a), F32)
    keep, send = pl.pallas_call(
        grams_kernel,
        out_shape=(piece, piece),
        grid=(rows // block,),
        in_specs=[
            SMEM,
            fixed(knot_order.shape),
            pl.BlockSpec((1, rows, block), lambda i: (0, 0, i)),
            fixed(basis_pool.shape),
            fixed(root_basis.shape),
            fixed(responses.shape),
        ],
        out_specs=(fixed(piece.shape), fixed(piece.shape)),
        scratch_shapes=[
            pltpu.VMEM((rows, wide_b), BF16),
            pltpu.VMEM((chips, 2, share, wide_b + wide_a), F32),
        ],
        name="grams",
    )(core_at, knot_order, leaf_factor, basis_pool, root_basis, responses)

    swap = [(i, i ^ 1) for i in range(leaf_count)]
    same_core = [list(range(c, leaf_count, 2)) for c in range(2)]
    paired = keep + lax.ppermute(send, "leaf", swap)
    arrived = lax.all_to_all(paired, "leaf", 0, 0, axis_index_groups=same_core, tiled=True)
    own = arrived.sum(axis=0)
    gathered = lax.all_gather(own[:, :wide_b], "leaf", axis=0, tiled=True)

    square = pltpu.VMEM((knots, knots), F32)
    small = [pltpu.VMEM((STEP, 128), F32), pltpu.VMEM((STEP, knots), F32)]
    obs = rows * leaf_count
    solved, schur, region_factor = pl.pallas_call(
        lambda *refs: region_kernel(1.0 / math.sqrt(obs), *refs),
        out_shape=(
            jax.ShapeDtypeStruct((knots, wide_a), F32),
            jax.ShapeDtypeStruct((share, wide_a), F32),
            jax.ShapeDtypeStruct((1, share, knots), F32),
        ),
        in_specs=[SMEM, VMEM, VMEM, VMEM],
        out_specs=(VMEM, VMEM, VMEM),
        scratch_shapes=[square, square, *small, pltpu.VMEM((roots, wide_a), F32)],
        name="region_solve",
    )(leaf_at, gathered, region_prior, own[:, wide_b:])

    copies = jnp.broadcast_to(schur[None], (region_count, *schur.shape))
    summed = lax.all_to_all(copies, "region", 0, 0, tiled=True).sum(axis=0)
    summed = lax.all_gather(summed, "leaf", axis=0, tiled=True)

    predictions, root_factor = pl.pallas_call(
        lambda *refs: root_kernel(1.0 / math.sqrt(obs * region_count), *refs),
        out_shape=(
            jax.ShapeDtypeStruct((1, rows, cols), BF16),
            jax.ShapeDtypeStruct((share, roots), F32),
        ),
        in_specs=[SMEM, VMEM, VMEM, VMEM, VMEM, ANY, ANY],
        out_specs=(VMEM, VMEM),
        scratch_shapes=[
            square, square, *small,
            pltpu.VMEM((rows, pool), BF16),
            pltpu.VMEM((rows, roots), BF16),
            pltpu.SemaphoreType.DMA((2,)),
        ],
        name="root_solve",
    )(leaf_at, summed, root_prior, solved, knot_order, basis_pool, root_basis)
    return predictions, region_factor, root_factor


def solution(mesh):
    placed = (
        P("region", "leaf", None),
        P("region", "leaf", None),
        P("region", "leaf", None),
        P("region", "leaf", None),
        P("region", None),
        P("region", None, None),
        P(),
    )
    return jax.shard_map(
        per_device,
        mesh=mesh,
        in_specs=placed,
        out_specs=(P("region", "leaf", None), P("region", "leaf", None), P("leaf", None)),
        check_vma=False,
    )
```

time: 385 us -> 182 us (0.47)
  the two profiles are of different devices: /device:TPU:8 before, /device:TPU:1 now
where the time goes in v1:
time: 182 us; the launch traced here: 181 us
  blocking collectives  127 us (70%)
  Pallas kernels  40.5 us (22%)
  starting transfers between devices  8.73 us (5%)
  waiting for transfers between devices  1.91 us (1%)
    all_to_all x1, blocking collectives, per_device(): lax.all_to_all(paired, 'leaf', 0, 0, axis_index_groups=same_core, tiled=T...  43.8 us
    all_gather x1, blocking collectives, per_device(): gathered = lax.all_gather(own[:, :wide_b], 'leaf', axis=0, tiled=True)  36.6 us
    all_gather x1, blocking collectives, per_device(): summed = lax.all_gather(summed, 'leaf', axis=0, tiled=True)  32.4 us
    pallas_call x1, Pallas kernels, per_device(): pl.pallas_call(lambda *refs: root_kernel(1.0 / math.sqrt(obs * region_cou...  17.2 us
    pallas_call x1, Pallas kernels, per_device(): pl.pallas_call(lambda *refs: region_kernel(1.0 / math.sqrt(obs), *refs),...  15.9 us
    all_to_all x1, blocking collectives, per_device(): summed = lax.all_to_all(copies, 'region', 0, 0, tiled=True).sum(axis=0)  14.3 us
    ppermute x1, starting transfers between devices, per_device(): paired = keep + lax.ppermute(send, 'leaf', swap)  8.73 us
    pallas_call x1, Pallas kernels, per_device(): pl.pallas_call(grams_kernel, out_shape=(piece, piece), grid=(rows // bloc...  7.37 us
  transfers between devices with their start and end apart: 1, of which 1 were waited for; matrix products, arithmetic and copies ran while one was open for 0% of the time, Pallas kernels for 0%

profile of v1, /device:TPU:1, one launch (start us, length us, event | category | flops | bytes accessed | tf_op | source)
XLA Modules:
  0.0 181.4 jit_solution(15140385438422515973)
XLA Ops:
  0.6 7.4 %grams.1 = (f32[16,8,1280]{2,1,0:T(8,128)}, f32[16,8,1280]{2,1,0:T(8,128)}) custom-call(s32[1]{0:T(128)} %bitcast.1.core_ref, s32[1,512]{1,0:T(1,128)} %refs_4_.1, bf16[1,1024,1024]{2,1,0:T(8,128)(2,1)} %factor_ref.1, bf16[1,1024,512]{2,1,0:T(8,128)(2,1)} %refs_5_.1, bf16[1,1024,256]{2,1,0:T(8,128)(2,1)} %refs_6_.1, bf16[1,1024,256]{2,1,0:T(8,128)(2,1)} %resp_ref.1), custom_call_target="tpu_custom_call" | custom-call | tf_op jit(solution)/shard_map/grams/pallas_call | solution.py:196
  8.0 8.7 %collective-permute-start = (f32[16,8,1280]{2,1,0:T(8,128)}, f32[16,8,1280]{2,1,0:T(8,128)S(1)}, u32[]{:S(2)}, u32[]{:S(2)}) collective-permute-start(f32[16,8,1280]{2,1,0:T(8,128)} %get-tuple-element.11), channel_id=1, source_target_pairs={{0,16},{16,0},{32,48},{48,32},{64,80},{80,64},{96,112},{112,96},{1... | collective-permute-start | bytes 1966088 | tf_op jit(solution)/shard_map/ppermute | solution.py:218
  16.8 1.9 %collective-permute-done = f32[16,8,1280]{2,1,0:T(8,128)S(1)} collective-permute-done((f32[16,8,1280]{2,1,0:T(8,128)}, f32[16,8,1280]{2,1,0:T(8,128)S(1)}, u32[]{:S(2)}, u32[]{:S(2)}) %collective-permute-start) | collective-permute-done | bytes 655392 | tf_op jit(solution)/shard_map/ppermute | solution.py:218
  18.7 1.2 add.3
  19.8 43.8 %all_to_all.10 = f32[16,8,1280]{2,1,0:T(8,128)S(1)} all-to-all(f32[16,8,1280]{2,1,0:T(8,128)S(1)} %add.3), channel_id=1, replica_groups={{0,32,64,96,128,160,192,224,256,288,320,352,384,416,448,480},{16,48,80,..., dimensions={0} | all-to-all | bytes 1310720 | tf_op jit(solution)/shard_map/all_to_all | solution.py:219
  63.6 0.6 slice.9.refs_3_
  64.3 36.6 %all_gather.6.refs_1_ = f32[256,768]{1,0:T(8,128)} all-gather(f32[8,768]{1,0:T(8,128)S(1)} %slice.8), channel_id=1, replica_groups=mesh['leaf'=32,'region'=16] {'leaf'}, dimensions={0}, use_global_device_ids=true | all-gather | bytes 811008 | tf_op jit(solution)/shard_map/all_gather | solution.py:221
  100.8 15.9 %region_solve.1 = (f32[256,512]{1,0:T(8,128)}, f32[8,512]{1,0:T(8,128)}, f32[1,8,256]{2,1,0:T(8,128)}) custom-call(s32[1]{0:T(128)} %bitcast.refs_0_, f32[256,768]{1,0:T(8,128)} %all_gather.6.refs_1_, bf16[1,256,256]{2,1,0:T(8,128)(2,1)} %refs_2_.2, f32[8,512]{1,0:T(8,128)} %slice.9.refs_3_), custom_call_target="tpu_custom_call" | custom-call | tf_op jit(solution)/shard_map/region_solve/pallas_call | solution.py:226
  116.7 0.7 broadcast_in_dim.2
  117.5 14.3 %all_to_all.11 = f32[16,8,512]{2,1,0:T(8,128)S(1)} all-to-all(f32[16,8,512]{2,1,0:T(8,128)S(1)} %broadcast_in_dim.2), channel_id=1, replica_groups=mesh['leaf'=32,'region'=16] {'region'}, dimensions={0} | all-to-all | bytes 524288 | tf_op jit(solution)/shard_map/all_to_all | solution.py:240
  131.8 32.4 %all_gather.7.refs_1_ = f32[256,512]{1,0:T(8,128)} all-gather(f32[8,512]{1,0:T(8,128)S(1)} %reduce_sum.19), channel_id=1, replica_groups=mesh['leaf'=32,'region'=16] {'leaf'}, dimensions={0}, use_global_device_ids=true | all-gather | bytes 540672 | tf_op jit(solution)/shard_map/all_gather | solution.py:241
  164.2 17.2 %root_solve.1 = (bf16[1,1024,256]{2,1,0:T(8,128)(2,1)}, f32[8,256]{1,0:T(8,128)}) custom-call(s32[1]{0:T(128)} %bitcast.refs_0_, f32[256,512]{1,0:T(8,128)} %all_gather.7.refs_1_, bf16[256,256]{1,0:T(8,128)(2,1)} %refs_2_.3, f32[256,512]{1,0:T(8,128)} %get-tuple-element.13.refs_3_, s32[1,512]{1,0:T(1,128)} %refs_4_.1, bf16[1,1024,512]{2,1,0:T(8,128)(2,1)} %refs_5_.1, ...), custom_call_target="tpu_custom_call" | custom-call | tf_op jit(solution)/shard_map/root_solve/pallas_call | solution.py:243
  (3 shorter events, 0.1 us)
Async XLA Ops:
  8.0 10.7 %collective-permute-start = (f32[16,8,1280]{2,1,0:T(8,128)}, f32[16,8,1280]{2,1,0:T(8,128)S(1)}, u32[]{:S(2)}, u32[]{:S(2)}) collective-permute-start(f32[16,8,1280]{2,1,0:T(8,128)} %get-tuple-element.11), channel_id=1, source_target_pairs={{0,16},{16,0},{32,48},{48,32},{64,80},{80,64},{96,112},{112,96},{1... | collective-permute-start | bytes 1966088 | tf_op jit(solution)/shard_map/ppermute | solution.py:218

commit v2 on v1

--- a/solution.py
+++ b/solution.py
@@ -26,7 +26,7 @@
 
 
 def grams_kernel(core_ref, knot_ref, factor_ref, pool_ref, root_ref, resp_ref,
-                 keep_ref, send_ref, joined, total):
+                 keep_b_ref, keep_a_ref, send_ref, joined, total):
     step = pl.program_id(0)
     knots = total.shape[2] * total.shape[0] * total.shape[1]
     roots = root_ref.shape[2]
@@ -50,8 +50,31 @@
     @pl.when(step == pl.num_programs(0) - 1)
     def _():
         core = core_ref[0]
-        keep_ref[...] = total[:, core]
+        keep = total[:, core]
+        keep_b_ref[...] = keep[:, :, : keep_b_ref.shape[2]]
+        keep_a_ref[...] = keep[:, :, keep_b_ref.shape[2] :]
         send_ref[...] = total[:, 1 - core]
+
+
+def pack_kernel(keep_ref, swapped_ref, arrived_ref, out_ref):
+    width = keep_ref.shape[2]
+    chips = out_ref.shape[0]
+    summed = arrived_ref[0]
+    for r in range(1, arrived_ref.shape[0]):
+        summed = summed + arrived_ref[r]
+    piece = summed.shape[1] // chips
+    out_ref[:, :, :width] = keep_ref[...] + swapped_ref[:, :, :width]
+    for z in range(chips):
+        out_ref[z, :, width : width + piece] = summed[:, z * piece : (z + 1) * piece]
+        rest = out_ref.shape[2] - width - piece
+        out_ref[z, :, width + piece :] = jnp.zeros((summed.shape[0], rest), F32)
+
+
+def spread_kernel(arrived_ref, own_ref, out_ref):
+    summed = arrived_ref[0]
+    for r in range(1, arrived_ref.shape[0]):
+        summed = summed + arrived_ref[r]
+    out_ref[...] = jnp.broadcast_to((own_ref[...] - summed)[None], out_ref.shape)
 
 
 def split3(x):
@@ -121,19 +144,27 @@
     return jnp.where(lane <= row, rows, 0.0) * scale
 
 
-def region_kernel(scale, leaf_ref, gathered_ref, prior_ref, own_ref,
-                  solved_ref, schur_ref, factor_ref, matrix, work, diag, panel, full):
+def region_kernel(scale, leaf_ref, gathered_ref, prior_ref,
+                  solved_ref, schur_ref, own_ref, factor_ref, matrix, work, diag, panel):
     size = matrix.shape[0]
     first = leaf_ref[0] * 8
+    width = size + solved_ref.shape[1]
     matrix[...] = prior_ref[0].astype(F32) + gathered_ref[:, :size]
     work[...] = matrix[...]
     inverse = factor_inverse(work, diag, panel)
-    half = jnp.dot(inverse, gathered_ref[:, size:], precision=HI, preferred_element_type=F32)
-    roots = full.shape[0]
-    full[...] = rows_dot(half[:, :roots], half, HI)
-    schur_ref[...] = own_ref[...] - full[pl.ds(pl.multiple_of(first, 8), 8), :]
+    half = jnp.dot(inverse, gathered_ref[:, size:width], precision=HI, preferred_element_type=F32)
+    schur = rows_dot(half[:, : schur_ref.shape[0] * schur_ref.shape[1]], half, HI)
+    schur_ref[...] = schur.reshape(schur_ref.shape)
     solved_ref[...] = rows_dot(inverse, half, HI)
     factor_ref[0] = factor_rows(matrix, first, inverse, scale)
+    chips = gathered_ref.shape[0] // 16
+    piece = own_ref.shape[1] // chips
+    for z in range(chips):
+        for core in range(2):
+            row = (2 * z + core) * 8
+            own_ref[core * 8 : core * 8 + 8, z * piece : (z + 1) * piece] = (
+                gathered_ref[row : row + 8, width : width + piece]
+            )
 
 
 def root_kernel(scale, leaf_ref, summed_ref, prior_ref, solved_ref, knot_ref, pool_hbm, root_hbm,
@@ -192,10 +223,17 @@
     def fixed(shape):
         return pl.BlockSpec(shape, lambda i: (0,) * len(shape))
 
-    piece = jax.ShapeDtypeStruct((chips, share, wide_b + wide_a), F32)
-    keep, send = pl.pallas_call(
+    def shape(*dims):
+        return jax.ShapeDtypeStruct(dims, F32)
+
+    pieces = (
+        shape(chips, share, wide_b),
+        shape(chips, share, wide_a),
+        shape(chips, share, wide_b + wide_a),
+    )
+    keep_b, keep_a, send = pl.pallas_call(
         grams_kernel,
-        out_shape=(piece, piece),
+        out_shape=pieces,
         grid=(rows // block,),
         in_specs=[
             SMEM,
@@ -205,7 +243,7 @@
             fixed(root_basis.shape),
             fixed(responses.shape),
         ],
-        out_specs=(fixed(piece.shape), fixed(piece.shape)),
+        out_specs=tuple(fixed(p.shape) for p in pieces),
         scratch_shapes=[
             pltpu.VMEM((rows, wide_b), BF16),
             pltpu.VMEM((chips, 2, share, wide_b + wide_a), F32),
@@ -215,30 +253,45 @@
 
     swap = [(i, i ^ 1) for i in range(leaf_count)]
     same_core = [list(range(c, leaf_count, 2)) for c in range(2)]
-    paired = keep + lax.ppermute(send, "leaf", swap)
-    arrived = lax.all_to_all(paired, "leaf", 0, 0, axis_index_groups=same_core, tiled=True)
-    own = arrived.sum(axis=0)
-    gathered = lax.all_gather(own[:, :wide_b], "leaf", axis=0, tiled=True)
+    swapped = lax.ppermute(send, "leaf", swap)
+    root_part = lax.all_to_all(keep_a + swapped[:, :, wide_b:], "region", 0, 0, tiled=True)
+    packed = pl.pallas_call(
+        pack_kernel,
+        out_shape=shape(chips, share, wide_b + 128),
+        in_specs=[VMEM, VMEM, VMEM],
+        out_specs=VMEM,
+        name="pack",
+    )(keep_b, swapped, root_part)
+    arrived = lax.all_to_all(packed, "leaf", 0, 0, axis_index_groups=same_core, tiled=True)
+    gathered = lax.all_gather(arrived.sum(axis=0), "leaf", axis=0, tiled=True)
 
     square = pltpu.VMEM((knots, knots), F32)
     small = [pltpu.VMEM((STEP, 128), F32), pltpu.VMEM((STEP, knots), F32)]
     obs = rows * leaf_count
-    solved, schur, region_factor = pl.pallas_call(
+    chunk = roots // region_count
+    solved, schur, own, region_factor = pl.pallas_call(
         lambda *refs: region_kernel(1.0 / math.sqrt(obs), *refs),
         out_shape=(
-            jax.ShapeDtypeStruct((knots, wide_a), F32),
-            jax.ShapeDtypeStruct((share, wide_a), F32),
-            jax.ShapeDtypeStruct((1, share, knots), F32),
+            shape(knots, wide_a),
+            shape(region_count, chunk, wide_a),
+            shape(chunk, wide_a),
+            shape(1, share, knots),
         ),
-        in_specs=[SMEM, VMEM, VMEM, VMEM],
-        out_specs=(VMEM, VMEM, VMEM),
-        scratch_shapes=[square, square, *small, pltpu.VMEM((roots, wide_a), F32)],
+        in_specs=[SMEM, VMEM, VMEM],
+        out_specs=(VMEM,) * 4,
+        scratch_shapes=[square, square, *small],
         name="region_solve",
-    )(leaf_at, gathered, region_prior, own[:, wide_b:])
-
-    copies = jnp.broadcast_to(schur[None], (region_count, *schur.shape))
-    summed = lax.all_to_all(copies, "region", 0, 0, tiled=True).sum(axis=0)
-    summed = lax.all_gather(summed, "leaf", axis=0, tiled=True)
+    )(leaf_at, gathered, region_prior)
+
+    schur = lax.all_to_all(schur, "region", 0, 0, tiled=True)
+    copies = pl.pallas_call(
+        spread_kernel,
+        out_shape=shape(region_count, chunk, wide_a),
+        in_specs=[VMEM, VMEM],
+        out_specs=VMEM,
+        name="spread",
+    )(schur, own)
+    summed = lax.all_to_all(copies, "region", 0, 0, tiled=True).reshape(roots, wide_a)
 
     predictions, root_factor = pl.pallas_call(
         lambda *refs: root_kernel(1.0 / math.sqrt(obs * region_count), *refs),

time: 182 us -> 173 us (0.951)
  blocking collectives: 127 us -> 115 us
  Pallas kernels: 40.5 us -> 44.4 us
    all_gather x2 -> x1, blocking collectives: 69 us -> 43 us  [per_device(): gathered = lax.all_gather(arrived.sum(axis=0), 'leaf', axis=0, tiled=True)]
    all_to_all x2 -> x4, blocking collectives: 58.1 us -> 71.6 us  [the longest x1 32.5 us: per_device(): lax.all_to_all(packed, 'leaf', 0, 0, axis_index_groups=same_core, tiled=T...]
    pallas_call x1 -> x3, Pallas kernels: 7.37 us -> 11.4 us  [the longest x1 7.38 us: per_device(): pl.pallas_call(grams_kernel, out_shape=pieces, grid=(rows // block,), in_...]
where the time goes in v2:
time: 173 us; the launch traced here: 171 us
  blocking collectives  115 us (66%)
  Pallas kernels  44.4 us (26%)
  starting transfers between devices  8.73 us (5%)
  waiting for transfers between devices  1.91 us (1%)
    all_gather x1, blocking collectives, per_device(): gathered = lax.all_gather(arrived.sum(axis=0), 'leaf', axis=0, tiled=True)  43 us
    all_to_all x1, blocking collectives, per_device(): lax.all_to_all(packed, 'leaf', 0, 0, axis_index_groups=same_core, tiled=T...  32.5 us
    pallas_call x1, Pallas kernels, per_device(): pl.pallas_call(lambda *refs: root_kernel(1.0 / math.sqrt(obs * region_cou...  17.2 us
    pallas_call x1, Pallas kernels, per_device(): pl.pallas_call(lambda *refs: region_kernel(1.0 / math.sqrt(obs), *refs),...  15.8 us
    all_to_all x1, blocking collectives, per_device(): schur = lax.all_to_all(schur, 'region', 0, 0, tiled=True)  14.6 us
    all_to_all x1, blocking collectives, per_device(): lax.all_to_all(copies, 'region', 0, 0, tiled=True).reshape(roots, wide_a)  13.4 us
    all_to_all x1, blocking collectives, per_device(): lax.all_to_all(keep_a + swapped[:, :, wide_b:], 'region', 0, 0, tiled=True)  11 us
    ppermute x1, starting transfers between devices, per_device(): swapped = lax.ppermute(send, 'leaf', swap)  8.73 us
  transfers between devices with their start and end apart: 1, of which 1 were waited for; matrix products, arithmetic and copies ran while one was open for 0% of the time, Pallas kernels for 0%

profile of v2, /device:TPU:1, one launch (start us, length us, event | category | flops | bytes accessed | tf_op | source)
XLA Modules:
  0.0 171.4 jit_solution(8294090880565388453)
XLA Ops:
  0.6 7.4 %grams.1 = (f32[16,8,768]{2,1,0:T(8,128)}, f32[16,8,512]{2,1,0:T(8,128)}, f32[16,8,1280]{2,1,0:T(8,128)}) custom-call(s32[1]{0:T(128)} %bitcast.1.core_ref, s32[1,512]{1,0:T(1,128)} %refs_4_.1, bf16[1,1024,1024]{2,1,0:T(8,128)(2,1)} %factor_ref.1, bf16[1,1024,512]{2,1,0:T(8,128)(2,1)} %refs_5_.1, bf16[1,1024,256]{2,1,0:T(8,128)(2,1)} %refs_6_.1, ...), custom_call_target="tpu_custom_call" | custom-call | tf_op jit(solution)/shard_map/grams/pallas_call | solution.py:234
  8.0 8.7 %collective-permute-start = (f32[16,8,1280]{2,1,0:T(8,128)}, f32[16,8,1280]{2,1,0:T(8,128)S(1)}, u32[]{:S(2)}, u32[]{:S(2)}) collective-permute-start(f32[16,8,1280]{2,1,0:T(8,128)} %get-tuple-element.13), channel_id=1, source_target_pairs={{0,16},{16,0},{32,48},{48,32},{64,80},{80,64},{96,112},{112,96},{1... | collective-permute-start | bytes 1966088 | tf_op jit(solution)/shard_map/ppermute | solution.py:256
  16.8 1.9 %collective-permute-done.swapped_ref = f32[16,8,1280]{2,1,0:T(8,128)S(1)} collective-permute-done((f32[16,8,1280]{2,1,0:T(8,128)}, f32[16,8,1280]{2,1,0:T(8,128)S(1)}, u32[]{:S(2)}, u32[]{:S(2)}) %collective-permute-start) | collective-permute-done | bytes 655392 | tf_op jit(solution)/shard_map/ppermute | solution.py:256
  18.7 0.0 copy-start
  18.7 1.1 slice_add_fusion
  19.8 11.0 %all_to_all.20.arrived_ref = f32[16,8,512]{2,1,0:T(8,128)} all-to-all(f32[16,8,512]{2,1,0:T(8,128)S(1)} %slice_add_fusion), channel_id=1, replica_groups=mesh['leaf'=32,'region'=16] {'region'}, dimensions={0} | all-to-all | bytes 524288 | tf_op jit(solution)/shard_map/all_to_all | solution.py:257
  30.8 0.0 copy-done
  30.8 2.1 %pack.1 = f32[16,8,896]{2,1,0:T(8,128)} custom-call(f32[16,8,768]{2,1,0:T(8,128)} %get-tuple-element.12.keep_ref, f32[16,8,1280]{2,1,0:T(8,128)} %copy-done, f32[16,8,512]{2,1,0:T(8,128)} %all_to_all.20.arrived_ref), custom_call_target="tpu_custom_call" | custom-call | tf_op jit(solution)/shard_map/pack/pallas_call | solution.py:258
  32.9 32.5 %all_to_all.21 = f32[16,8,896]{2,1,0:T(8,128)S(1)} all-to-all(f32[16,8,896]{2,1,0:T(8,128)} %pack.1), channel_id=1, replica_groups={{0,32,64,96,128,160,192,224,256,288,320,352,384,416,448,480},{16,48,80,..., dimensions={0} | all-to-all | bytes 917504 | tf_op jit(solution)/shard_map/all_to_all | solution.py:265
  65.5 43.0 %all_gather.3.refs_1_ = f32[256,896]{1,0:T(8,128)} all-gather(f32[8,896]{1,0:T(8,128)S(1)} %reduce_sum.9), channel_id=1, replica_groups=mesh['leaf'=32,'region'=16] {'leaf'}, dimensions={0}, use_global_device_ids=true | all-gather | bytes 946176 | tf_op jit(solution)/shard_map/all_gather | solution.py:266
  108.5 15.8 %region_solve.1 = (f32[256,512]{1,0:T(8,128)}, f32[16,16,512]{2,1,0:T(8,128)}, f32[16,512]{1,0:T(8,128)}, f32[1,8,256]{2,1,0:T(8,128)}) custom-call(s32[1]{0:T(128)} %bitcast.refs_0_, f32[256,896]{1,0:T(8,128)} %all_gather.3.refs_1_, bf16[1,256,256]{2,1,0:T(8,128)(2,1)} %refs_2_.2), custom_call_target="tpu_custom_call" | custom-call | tf_op jit(solution)/shard_map/region_solve/pallas_call | solution.py:272
  124.3 14.6 %all_to_all.22.arrived_ref = f32[16,16,512]{2,1,0:T(8,128)} all-to-all(f32[16,16,512]{2,1,0:T(8,128)} %get-tuple-element.15), channel_id=1, replica_groups=mesh['leaf'=32,'region'=16] {'region'}, dimensions={0} | all-to-all | bytes 1048576 | tf_op jit(solution)/shard_map/all_to_all | solution.py:286
  138.9 1.9 %spread.1 = f32[16,16,512]{2,1,0:T(8,128)} custom-call(f32[16,16,512]{2,1,0:T(8,128)} %all_to_all.22.arrived_ref, f32[16,512]{1,0:T(8,128)} %get-tuple-element.16.own_ref), custom_call_target="tpu_custom_call" | custom-call | tf_op jit(solution)/shard_map/spread/pallas_call | solution.py:287
  140.8 13.4 %all_to_all.23 = f32[16,16,512]{2,1,0:T(8,128)} all-to-all(f32[16,16,512]{2,1,0:T(8,128)} %spread.1), channel_id=1, replica_groups=mesh['leaf'=32,'region'=16] {'region'}, dimensions={0} | all-to-all | bytes 1048576 | tf_op jit(solution)/shard_map/all_to_all | solution.py:294
  154.3 17.2 %root_solve.1 = (bf16[1,1024,256]{2,1,0:T(8,128)(2,1)}, f32[8,256]{1,0:T(8,128)}) custom-call(s32[1]{0:T(128)} %bitcast.refs_0_, f32[256,512]{1,0:T(8,128)} %bitcast.3, bf16[256,256]{1,0:T(8,128)(2,1)} %refs_2_.3, f32[256,512]{1,0:T(8,128)} %get-tuple-element.17.refs_3_, s32[1,512]{1,0:T(1,128)} %refs_4_.1, bf16[1,1024,512]{2,1,0:T(8,128)(2,1)} %refs_5_.1, ...), custom_call_target="tpu_custom_call" | custom-call | tf_op jit(solution)/shard_map/root_solve/pallas_call | solution.py:296
  (1 shorter events, 0.0 us)
Async XLA Ops:
  8.0 10.7 %collective-permute-start = (f32[16,8,1280]{2,1,0:T(8,128)}, f32[16,8,1280]{2,1,0:T(8,128)S(1)}, u32[]{:S(2)}, u32[]{:S(2)}) collective-permute-start(f32[16,8,1280]{2,1,0:T(8,128)} %get-tuple-element.13), channel_id=1, source_target_pairs={{0,16},{16,0},{32,48},{48,32},{64,80},{80,64},{96,112},{112,96},{1... | collective-permute-start | bytes 1966088 | tf_op jit(solution)/shard_map/ppermute | solution.py:256
  18.7 12.1 %copy-start = (f32[16,8,1280]{2,1,0:T(8,128)}, f32[16,8,1280]{2,1,0:T(8,128)S(1)}, u32[]{:S(2)}) copy-start(f32[16,8,1280]{2,1,0:T(8,128)S(1)} %collective-permute-done.swapped_ref) | copy-start | bytes 1966084

commit v3 on v2

--- a/solution.py
+++ b/solution.py
@@ -26,10 +26,11 @@
 
 
 def grams_kernel(core_ref, knot_ref, factor_ref, pool_ref, root_ref, resp_ref,
-                 keep_b_ref, keep_a_ref, send_ref, joined, total):
+                 keep_b_ref, keep_a_ref, send_ref, joined, total_b, total_a):
     step = pl.program_id(0)
-    knots = total.shape[2] * total.shape[0] * total.shape[1]
+    width = total_b.shape[3]
     roots = root_ref.shape[2]
+    knots = width - total_a.shape[3]
 
     @pl.when(step == 0)
     def _():
@@ -38,22 +39,22 @@
         joined[:, :knots] = basis.astype(BF16)
         joined[:, knots : knots + roots] = root_ref[0]
         joined[:, knots + roots :] = resp_ref[0]
-        total[...] = jnp.zeros_like(total)
+        total_b[...] = jnp.zeros_like(total_b)
+        total_a[...] = jnp.zeros_like(total_a)
 
     white = rows_dot(factor_ref[0], joined[...]).astype(BF16)
-    gram_b = rows_dot(white[:, :knots], white)
-    gram_a = rows_dot(white[:, knots : knots + roots], white[:, knots:])
-    width = gram_b.shape[1]
-    total[:, :, :, :width] += gram_b.reshape(*total.shape[:3], width)
-    total[:, :, :, width:] += gram_a.reshape(*total.shape[:3], gram_a.shape[1])
+    total_b[...] += rows_dot(white[:, :knots], white).reshape(total_b.shape)
+    total_a[...] += rows_dot(white[:, knots : knots + roots], white[:, knots:]).reshape(
+        total_a.shape
+    )
 
     @pl.when(step == pl.num_programs(0) - 1)
     def _():
         core = core_ref[0]
-        keep = total[:, core]
-        keep_b_ref[...] = keep[:, :, : keep_b_ref.shape[2]]
-        keep_a_ref[...] = keep[:, :, keep_b_ref.shape[2] :]
-        send_ref[...] = total[:, 1 - core]
+        keep_b_ref[...] = total_b[core]
+        keep_a_ref[...] = total_a[:, core]
+        send_ref[:, :, :width] = total_b[1 - core]
+        send_ref[:, :, width:] = total_a[:, 1 - core]
 
 
 def pack_kernel(keep_ref, swapped_ref, arrived_ref, out_ref):
@@ -85,33 +86,50 @@
     return high, mid, low
 
 
+def split_dot(left, right, dims, terms=6):
+    lh, lm, ll = split3(left)
+    rh, rm, rl = split3(right)
+    lefts = jnp.concatenate([lh, lh, lm, lh, ll, lm][:terms], axis=dims[0])
+    rights = jnp.concatenate([rh, rm, rh, rl, rh, rm][:terms], axis=dims[1])
+    return lax.dot_general(
+        lefts, rights, (((dims[0],), (dims[1],)), ((), ())), preferred_element_type=F32
+    )
+
+
 def factor_inverse(work, diag, panel):
     size = work.shape[0]
+    tiles = size // 128
 
     def block(k, _):
         start = pl.multiple_of(k * STEP, STEP)
         tile = pl.multiple_of((start // 128) * 128, 128)
         corner = work[pl.ds(start, STEP), pl.ds(tile, 128)]
         diag[...] = pltpu.roll(corner, lax.rem(128 - (start - tile), 128), 1)
-        lane = lax.broadcasted_iota(jnp.int32, (8, size), 1)
-        inside = (lane >= start) & (lane < start + STEP)
+        held = work[pl.ds(start, STEP), :]
+        sub = lax.broadcasted_iota(jnp.int32, (8, 128), 0)
+        at = sub * 128 + lax.broadcasted_iota(jnp.int32, (8, 128), 1) - start
+        inside = (at >= 0) & (at < STEP)
         d, v = [], []
         for i in range(STEP):
             row = jnp.broadcast_to(diag[i : i + 1, :], (8, 128))
             d.append([None] * i + [jnp.broadcast_to(row[:, j : j + 1], (8, 128)) for j in range(i, STEP)])
-            full = jnp.broadcast_to(work[pl.ds(start + i, 1), :], (8, size))
-            v.append(jnp.where(inside, jnp.where(lane == start + i, 1.0, 0.0), full))
+            full = jnp.broadcast_to(held[i : i + 1, 0:128], (8, 128))
+            for t in range(1, tiles):
+                more = held[i : i + 1, t * 128 : (t + 1) * 128]
+                full = jnp.where(sub == t, jnp.broadcast_to(more, (8, 128)), full)
+            v.append(jnp.where(inside, jnp.where(at == i, 1.0, 0.0), full))
         for p in range(STEP):
             scale = lax.rsqrt(d[p][p])
             u = [None] * (p + 1) + [d[p][j] * scale for j in range(p + 1, STEP)]
-            wide = jnp.concatenate([scale] * (size // 128), axis=1)
-            done = v[p] * wide
-            panel[p : p + 1, :] = done[0:1, :]
+            done = v[p] * scale
+            panel[tiles * p : tiles * (p + 1), :] = done[0:tiles, :]
             for i in range(p + 1, STEP):
                 for j in range(i, STEP):
                     d[i][j] = d[i][j] - u[i] * u[j]
-                v[i] = v[i] - jnp.concatenate([u[i]] * (size // 128), axis=1) * done
-        rows = panel[...]
+                v[i] = v[i] - u[i] * done
+        rows = jnp.concatenate(
+            [panel[pl.ds(t, STEP, stride=tiles), :] for t in range(tiles)], axis=1
+        )
         lane_p = lax.broadcasted_iota(jnp.int32, (STEP, size), 1)
         high, mid, low = split3(rows)
         later = lane_p >= start + STEP
@@ -136,9 +154,7 @@
 def factor_rows(matrix, first, inverse, scale):
     count = 8
     part = matrix[pl.ds(pl.multiple_of(first, 8), count), :]
-    rows = lax.dot_general(
-        part, inverse, (((1,), (1,)), ((), ())), precision=HI, preferred_element_type=F32
-    )
+    rows = split_dot(part, inverse, (1, 1), 3)
     lane = lax.broadcasted_iota(jnp.int32, rows.shape, 1)
     row = lax.broadcasted_iota(jnp.int32, rows.shape, 0) + first
     return jnp.where(lane <= row, rows, 0.0) * scale
@@ -152,16 +168,16 @@
     matrix[...] = prior_ref[0].astype(F32) + gathered_ref[:, :size]
     work[...] = matrix[...]
     inverse = factor_inverse(work, diag, panel)
-    half = jnp.dot(inverse, gathered_ref[:, size:width], precision=HI, preferred_element_type=F32)
-    schur = rows_dot(half[:, : schur_ref.shape[0] * schur_ref.shape[1]], half, HI)
+    half = split_dot(inverse, gathered_ref[:, size:width], (1, 0))
+    schur = split_dot(half[:, : schur_ref.shape[0] * schur_ref.shape[1]], half, (0, 0))
     schur_ref[...] = schur.reshape(schur_ref.shape)
-    solved_ref[...] = rows_dot(inverse, half, HI)
+    solved_ref[...] = split_dot(inverse, half, (0, 0), 3)
     factor_ref[0] = factor_rows(matrix, first, inverse, scale)
     chips = gathered_ref.shape[0] // 16
     piece = own_ref.shape[1] // chips
     for z in range(chips):
         for core in range(2):
-            row = (2 * z + core) * 8
+            row = (core * chips + z) * 8
             own_ref[core * 8 : core * 8 + 8, z * piece : (z + 1) * piece] = (
                 gathered_ref[row : row + 8, width : width + piece]
             )
@@ -180,11 +196,9 @@
     matrix[...] = prior_ref[...].astype(F32) + summed_ref[:, :size]
     work[...] = matrix[...]
     inverse = factor_inverse(work, diag, panel)
-    half = jnp.dot(inverse, summed_ref[:, size:], precision=HI, preferred_element_type=F32)
-    root_coef = rows_dot(inverse, half, HI)
-    coef = solved_ref[:, size:] - jnp.dot(
-        solved_ref[:, :size], root_coef, precision=HI, preferred_element_type=F32
-    )
+    half = split_dot(inverse, summed_ref[:, size:], (1, 0), 3)
+    root_coef = split_dot(inverse, half, (0, 0), 3)
+    coef = solved_ref[:, size:] - split_dot(solved_ref[:, :size], root_coef, (1, 0), 3)
     knots = coef.shape[0]
     pick = one_hot(knot_ref[:, :knots], pool.shape[1])
     spread = jnp.dot(pick, coef.astype(BF16), preferred_element_type=F32).astype(BF16)
@@ -246,7 +260,8 @@
         out_specs=tuple(fixed(p.shape) for p in pieces),
         scratch_shapes=[
             pltpu.VMEM((rows, wide_b), BF16),
-            pltpu.VMEM((chips, 2, share, wide_b + wide_a), F32),
+            pltpu.VMEM((2, chips, share, wide_b), F32),
+            pltpu.VMEM((chips, 2, share, wide_a), F32),
         ],
         name="grams",
     )(core_at, knot_order, leaf_factor, basis_pool, root_basis, responses)
@@ -263,10 +278,14 @@
         name="pack",
     )(keep_b, swapped, root_part)
     arrived = lax.all_to_all(packed, "leaf", 0, 0, axis_index_groups=same_core, tiled=True)
-    gathered = lax.all_gather(arrived.sum(axis=0), "leaf", axis=0, tiled=True)
+    copies = jnp.broadcast_to(arrived.sum(axis=0)[None], arrived.shape)
+    column = lax.all_to_all(copies, "leaf", 0, 0, axis_index_groups=same_core, tiled=True)
+    column = column.reshape(chips * share, column.shape[2])
+    same_chip = [[i, i + 1] for i in range(0, leaf_count, 2)]
+    gathered = lax.all_gather(column, "leaf", axis=0, axis_index_groups=same_chip, tiled=True)
 
     square = pltpu.VMEM((knots, knots), F32)
-    small = [pltpu.VMEM((STEP, 128), F32), pltpu.VMEM((STEP, knots), F32)]
+    small = [pltpu.VMEM((STEP, 128), F32), pltpu.VMEM((STEP * knots // 128, 128), F32)]
     obs = rows * leaf_count
     chunk = roots // region_count
     solved, schur, own, region_factor = pl.pallas_call(

time: 173 us -> 169 us (0.977)
  Pallas kernels: 44.4 us -> 42.2 us
  blocking collectives: 115 us -> 113 us
    all_gather x1, blocking collectives: 43 us -> 8.28 us  [per_device(): lax.all_gather(column, 'leaf', axis=0, axis_index_groups=same_chip, tiled...]
    all_to_all x0 -> x1, blocking collectives: none -> 32.3 us  [per_device(): lax.all_to_all(copies, 'leaf', 0, 0, axis_index_groups=same_core, tiled=T...]
where the time goes in v3:
time: 169 us; the launch traced here: 167 us
  blocking collectives  113 us (67%)
  Pallas kernels  42.2 us (25%)
  starting transfers between devices  8.73 us (5%)
  waiting for transfers between devices  1.91 us (1%)
    all_to_all x1, blocking collectives, per_device(): lax.all_to_all(packed, 'leaf', 0, 0, axis_index_groups=same_core, tiled=T...  32.5 us
    all_to_all x1, blocking collectives, per_device(): lax.all_to_all(copies, 'leaf', 0, 0, axis_index_groups=same_core, tiled=T...  32.3 us
    pallas_call x1, Pallas kernels, per_device(): pl.pallas_call(lambda *refs: root_kernel(1.0 / math.sqrt(obs * region_cou...  15.7 us
    all_to_all x1, blocking collectives, per_device(): schur = lax.all_to_all(schur, 'region', 0, 0, tiled=True)  15.3 us
    pallas_call x1, Pallas kernels, per_device(): pl.pallas_call(lambda *refs: region_kernel(1.0 / math.sqrt(obs), *refs),...  15 us
    all_to_all x1, blocking collectives, per_device(): lax.all_to_all(copies, 'region', 0, 0, tiled=True).reshape(roots, wide_a)  13.4 us
    all_to_all x1, blocking collectives, per_device(): lax.all_to_all(keep_a + swapped[:, :, wide_b:], 'region', 0, 0, tiled=True)  11 us
    ppermute x1, starting transfers between devices, per_device(): swapped = lax.ppermute(send, 'leaf', swap)  8.73 us
  transfers between devices with their start and end apart: 1, of which 1 were waited for; matrix products, arithmetic and copies ran while one was open for 0% of the time, Pallas kernels for 0%

profile of v3, /device:TPU:1, one launch (start us, length us, event | category | flops | bytes accessed | tf_op | source)
XLA Modules:
  0.0 167.5 jit_solution(7163453749460859646)
XLA Ops:
  0.6 7.4 %grams.1 = (f32[16,8,768]{2,1,0:T(8,128)}, f32[16,8,512]{2,1,0:T(8,128)}, f32[16,8,1280]{2,1,0:T(8,128)}) custom-call(s32[1]{0:T(128)} %bitcast.1.core_ref, s32[1,512]{1,0:T(1,128)} %refs_4_.1, bf16[1,1024,1024]{2,1,0:T(8,128)(2,1)} %factor_ref.1, bf16[1,1024,512]{2,1,0:T(8,128)(2,1)} %refs_5_.1, bf16[1,1024,256]{2,1,0:T(8,128)(2,1)} %refs_6_.1, ...), custom_call_target="tpu_custom_call" | custom-call | tf_op jit(solution)/shard_map/grams/pallas_call | solution.py:248
  8.0 8.7 %collective-permute-start = (f32[16,8,1280]{2,1,0:T(8,128)}, f32[16,8,1280]{2,1,0:T(8,128)S(1)}, u32[]{:S(2)}, u32[]{:S(2)}) collective-permute-start(f32[16,8,1280]{2,1,0:T(8,128)} %get-tuple-element.13), channel_id=1, source_target_pairs={{0,16},{16,0},{32,48},{48,32},{64,80},{80,64},{96,112},{112,96},{1... | collective-permute-start | bytes 1966088 | tf_op jit(solution)/shard_map/ppermute | solution.py:271
  16.7 1.9 %collective-permute-done.swapped_ref = f32[16,8,1280]{2,1,0:T(8,128)S(1)} collective-permute-done((f32[16,8,1280]{2,1,0:T(8,128)}, f32[16,8,1280]{2,1,0:T(8,128)S(1)}, u32[]{:S(2)}, u32[]{:S(2)}) %collective-permute-start) | collective-permute-done | bytes 655392 | tf_op jit(solution)/shard_map/ppermute | solution.py:271
  18.7 0.0 copy-start
  18.7 1.1 slice_add_fusion
  19.8 11.0 %all_to_all.25.arrived_ref = f32[16,8,512]{2,1,0:T(8,128)} all-to-all(f32[16,8,512]{2,1,0:T(8,128)S(1)} %slice_add_fusion), channel_id=1, replica_groups=mesh['leaf'=32,'region'=16] {'region'}, dimensions={0} | all-to-all | bytes 524288 | tf_op jit(solution)/shard_map/all_to_all | solution.py:272
  30.8 0.0 copy-done
  30.8 2.1 %pack.1 = f32[16,8,896]{2,1,0:T(8,128)} custom-call(f32[16,8,768]{2,1,0:T(8,128)} %get-tuple-element.12.keep_ref, f32[16,8,1280]{2,1,0:T(8,128)} %copy-done, f32[16,8,512]{2,1,0:T(8,128)} %all_to_all.25.arrived_ref), custom_call_target="tpu_custom_call" | custom-call | tf_op jit(solution)/shard_map/pack/pallas_call | solution.py:273
  32.9 32.5 %all_to_all.26 = f32[16,8,896]{2,1,0:T(8,128)S(1)} all-to-all(f32[16,8,896]{2,1,0:T(8,128)} %pack.1), channel_id=1, replica_groups={{0,32,64,96,128,160,192,224,256,288,320,352,384,416,448,480},{16,48,80,..., dimensions={0} | all-to-all | bytes 917504 | tf_op jit(solution)/shard_map/all_to_all | solution.py:280
  65.5 32.3 %all_to_all.27 = f32[16,8,896]{2,1,0:T(8,128)S(1)} all-to-all(f32[16,8,896]{2,1,0:T(8,128)S(1)} %broadcast_in_dim.2), channel_id=1, replica_groups={{0,32,64,96,128,160,192,224,256,288,320,352,384,416,448,480},{16,48,80,..., dimensions={0} | all-to-all | bytes 917504 | tf_op jit(solution)/shard_map/all_to_all | solution.py:282
  97.8 8.3 %all_gather.3.refs_1_ = f32[256,896]{1,0:T(8,128)} all-gather(f32[128,896]{1,0:T(8,128)S(1)} %bitcast.5), channel_id=1, replica_groups={{0,16},{32,48},{64,80},{96,112},{128,144},{160,176},{192,208},{224,240}..., dimensions={0}, use_global_device_ids=true | all-gather | bytes 1376256 | tf_op jit(solution)/shard_map/all_gather | solution.py:285
  106.1 15.0 %region_solve.1 = (f32[256,512]{1,0:T(8,128)}, f32[16,16,512]{2,1,0:T(8,128)}, f32[16,512]{1,0:T(8,128)}, f32[1,8,256]{2,1,0:T(8,128)}) custom-call(s32[1]{0:T(128)} %bitcast.refs_0_, f32[256,896]{1,0:T(8,128)} %all_gather.3.refs_1_, bf16[1,256,256]{2,1,0:T(8,128)(2,1)} %refs_2_.2), custom_call_target="tpu_custom_call" | custom-call | tf_op jit(solution)/shard_map/region_solve/pallas_call | solution.py:291
  121.1 15.3 %all_to_all.28.arrived_ref = f32[16,16,512]{2,1,0:T(8,128)} all-to-all(f32[16,16,512]{2,1,0:T(8,128)} %get-tuple-element.15), channel_id=1, replica_groups=mesh['leaf'=32,'region'=16] {'region'}, dimensions={0} | all-to-all | bytes 1048576 | tf_op jit(solution)/shard_map/all_to_all | solution.py:305
  136.4 1.9 %spread.1 = f32[16,16,512]{2,1,0:T(8,128)} custom-call(f32[16,16,512]{2,1,0:T(8,128)} %all_to_all.28.arrived_ref, f32[16,512]{1,0:T(8,128)} %get-tuple-element.16.own_ref), custom_call_target="tpu_custom_call" | custom-call | tf_op jit(solution)/shard_map/spread/pallas_call | solution.py:306
  138.3 13.4 %all_to_all.29 = f32[16,16,512]{2,1,0:T(8,128)} all-to-all(f32[16,16,512]{2,1,0:T(8,128)} %spread.1), channel_id=1, replica_groups=mesh['leaf'=32,'region'=16] {'region'}, dimensions={0} | all-to-all | bytes 1048576 | tf_op jit(solution)/shard_map/all_to_all | solution.py:313
  151.7 15.7 %root_solve.1 = (bf16[1,1024,256]{2,1,0:T(8,128)(2,1)}, f32[8,256]{1,0:T(8,128)}) custom-call(s32[1]{0:T(128)} %bitcast.refs_0_, f32[256,512]{1,0:T(8,128)} %bitcast.4, bf16[256,256]{1,0:T(8,128)(2,1)} %refs_2_.3, f32[256,512]{1,0:T(8,128)} %get-tuple-element.17.refs_3_, s32[1,512]{1,0:T(1,128)} %refs_4_.1, bf16[1,1024,512]{2,1,0:T(8,128)(2,1)} %refs_5_.1, ...), custom_call_target="tpu_custom_call" | custom-call | tf_op jit(solution)/shard_map/root_solve/pallas_call | solution.py:315
  (2 shorter events, 0.1 us)
Async XLA Ops:
  8.0 10.7 %collective-permute-start = (f32[16,8,1280]{2,1,0:T(8,128)}, f32[16,8,1280]{2,1,0:T(8,128)S(1)}, u32[]{:S(2)}, u32[]{:S(2)}) collective-permute-start(f32[16,8,1280]{2,1,0:T(8,128)} %get-tuple-element.13), channel_id=1, source_target_pairs={{0,16},{16,0},{32,48},{48,32},{64,80},{80,64},{96,112},{112,96},{1... | collective-permute-start | bytes 1966088 | tf_op jit(solution)/shard_map/ppermute | solution.py:271
  18.7 12.1 %copy-start = (f32[16,8,1280]{2,1,0:T(8,128)}, f32[16,8,1280]{2,1,0:T(8,128)S(1)}, u32[]{:S(2)}) copy-start(f32[16,8,1280]{2,1,0:T(8,128)S(1)} %collective-permute-done.swapped_ref) | copy-start | bytes 1966084

commit v4 on v1

v4 whole, which is shorter than its diff:
```python
import math

import jax
import jax.numpy as jnp
from jax import lax
from jax.experimental import pallas as pl
from jax.experimental.pallas import tpu as pltpu
from jax.sharding import PartitionSpec as P

STEP = 16
HI = lax.Precision.HIGHEST
F32 = jnp.float32
BF16 = jnp.bfloat16


def rows_dot(left, right, precision=None):
    return lax.dot_general(
        left, right, (((0,), (0,)), ((), ())), precision=precision, preferred_element_type=F32
    )


def one_hot(knots, pool):
    count = knots.shape[1]
    ids = lax.broadcasted_iota(jnp.int32, (pool, count), 0)
    return (ids == knots).astype(BF16)


def grams_kernel(core_ref, knot_ref, factor_hbm, pool_hbm, root_hbm, resp_hbm,
                 keep_ref, send_ref, joined, factor, pool, total, sems):
    roots = root_hbm.shape[2]
    width = joined.shape[1]
    knots = width - roots - resp_hbm.shape[2]
    loads = [
        pltpu.make_async_copy(pool_hbm.at[0], pool, sems.at[0]),
        pltpu.make_async_copy(root_hbm.at[0], joined.at[:, pl.ds(knots, roots)], sems.at[1]),
        pltpu.make_async_copy(
            resp_hbm.at[0], joined.at[:, pl.ds(knots + roots, width - knots - roots)], sems.at[2]
        ),
        pltpu.make_async_copy(factor_hbm.at[0], factor, sems.at[3]),
    ]
    for load in loads:
        load.start()
    pick = one_hot(knot_ref[:, :knots], pool.shape[1])
    loads[0].wait()
    basis = jnp.dot(pool[...], pick, preferred_element_type=F32)
    joined[:, :knots] = basis.astype(BF16)
    for load in loads[1:]:
        load.wait()
    white = rows_dot(factor[...], joined[...]).astype(BF16)
    gram_b = rows_dot(white[:, :knots], white)
    gram_a = rows_dot(white[:, knots : knots + roots], white[:, knots:])
    total[:, :, :, :width] = gram_b.reshape(*total.shape[:3], width)
    total[:, :, :, width:] = gram_a.reshape(*total.shape[:3], gram_a.shape[1])
    core = core_ref[0]
    keep_ref[...] = total[core]
    send_ref[...] = total[1 - core]


def split3(x):
    high = x.astype(BF16)
    rest = x - high.astype(F32)
    mid = rest.astype(BF16)
    low = (rest - mid.astype(F32)).astype(BF16)
    return high, mid, low


def split_dot(left, right, dims, terms=6):
    lh, lm, ll = split3(left)
    rh, rm, rl = split3(right)
    lefts = jnp.concatenate([lh, lh, lm, lh, ll, lm][:terms], axis=dims[0])
    rights = jnp.concatenate([rh, rm, rh, rl, rh, rm][:terms], axis=dims[1])
    return lax.dot_general(
        lefts, rights, (((dims[0],), (dims[1],)), ((), ())), preferred_element_type=F32
    )


def factor_inverse(work, diag, panel):
    size = work.shape[0]
    tiles = size // 128

    def block(k, _):
        start = pl.multiple_of(k * STEP, STEP)
        tile = pl.multiple_of((start // 128) * 128, 128)
        corner = work[pl.ds(start, STEP), pl.ds(tile, 128)]
        diag[...] = pltpu.roll(corner, lax.rem(128 - (start - tile), 128), 1)
        held = work[pl.ds(start, STEP), :]
        sub = lax.broadcasted_iota(jnp.int32, (8, 128), 0)
        at = sub * 128 + lax.broadcasted_iota(jnp.int32, (8, 128), 1) - start
        inside = (at >= 0) & (at < STEP)
        d, v = [], []
        for i in range(STEP):
            row = jnp.broadcast_to(diag[i : i + 1, :], (8, 128))
            d.append([None] * i + [jnp.broadcast_to(row[:, j : j + 1], (8, 128)) for j in range(i, STEP)])
            full = jnp.broadcast_to(held[i : i + 1, 0:128], (8, 128))
            for t in range(1, tiles):
                more = held[i : i + 1, t * 128 : (t + 1) * 128]
                full = jnp.where(sub == t, jnp.broadcast_to(more, (8, 128)), full)
            v.append(jnp.where(inside, jnp.where(at == i, 1.0, 0.0), full))
        for p in range(STEP):
            scale = lax.rsqrt(d[p][p])
            u = [None] * (p + 1) + [d[p][j] * scale for j in range(p + 1, STEP)]
            done = v[p] * scale
            panel[tiles * p : tiles * (p + 1), :] = done[0:tiles, :]
            for i in range(p + 1, STEP):
                for j in range(i, STEP):
                    d[i][j] = d[i][j] - u[i] * u[j]
                v[i] = v[i] - u[i] * done
        rows = jnp.concatenate(
            [panel[pl.ds(t, STEP, stride=tiles), :] for t in range(tiles)], axis=1
        )
        lane_p = lax.broadcasted_iota(jnp.int32, (STEP, size), 1)
        high, mid, low = split3(rows)
        later = lane_p >= start + STEP
        zero = jnp.zeros_like(high)
        th, tm, tl = (jnp.where(later, x, zero) for x in (high, mid, low))
        left = jnp.concatenate([th, th, tm, th, tl, tm], axis=0)
        right = jnp.concatenate([high, mid, high, low, high, mid], axis=0)
        change = rows_dot(left, right)
        lane_a = lax.broadcasted_iota(jnp.int32, (size, size), 1)
        row_a = lax.broadcasted_iota(jnp.int32, (size, size), 0)
        fresh = (lane_a >= start) & (lane_a < start + STEP) & (row_a >= start + STEP)
        work[...] = jnp.where(fresh, 0.0, work[...]) - change
        work[pl.ds(start, STEP), :] = rows
        return 0

    lax.fori_loop(0, size // STEP, block, 0)
    lane = lax.broadcasted_iota(jnp.int32, (size, size), 1)
    row = lax.broadcasted_iota(jnp.int32, (size, size), 0)
    return jnp.where(lane <= row, work[...], 0.0)


def factor_rows(matrix, first, inverse, scale):
    count = 8
    part = matrix[pl.ds(pl.multiple_of(first, 8), count), :]
    rows = split_dot(part, inverse, (1, 1), 3)
    lane = lax.broadcasted_iota(jnp.int32, rows.shape, 1)
    row = lax.broadcasted_iota(jnp.int32, rows.shape, 0) + first
    return jnp.where(lane <= row, rows, 0.0) * scale


def region_kernel(scale, leaf_ref, gathered_ref, column_ref, prior_ref,
                  solved_ref, schur_ref, factor_ref, matrix, work, diag, panel, half_ref):
    size = matrix.shape[0]
    first = leaf_ref[0] * 8
    width = size + solved_ref.shape[1]
    count = schur_ref.shape[0] * schur_ref.shape[1]
    mine = pl.multiple_of(lax.rem(leaf_ref[0], 2) * count, count)
    matrix[...] = prior_ref[0].astype(F32) + gathered_ref[:, :size]
    work[...] = matrix[...]
    inverse = factor_inverse(work, diag, panel)
    half = split_dot(inverse, gathered_ref[:, size:width], (1, 0))
    half_ref[...] = half
    schur = column_ref[:, width:] - split_dot(
        half_ref[:, pl.ds(mine, count)], half, (0, 0)
    )
    schur_ref[...] = schur.reshape(schur_ref.shape)
    solved_ref[...] = split_dot(inverse, half, (0, 0), 3)
    factor_ref[0] = factor_rows(matrix, first, inverse, scale)


def root_kernel(scale, leaf_ref, summed_ref, prior_ref, solved_ref, knot_ref, pool_hbm, root_hbm,
                pred_ref, factor_ref, matrix, work, diag, panel, pool, root, sems):
    size = matrix.shape[0]
    loads = [
        pltpu.make_async_copy(pool_hbm.at[0], pool, sems.at[0]),
        pltpu.make_async_copy(root_hbm.at[0], root, sems.at[1]),
    ]
    for load in loads:
        load.start()
    first = leaf_ref[0] * 8
    matrix[...] = prior_ref[...].astype(F32) + summed_ref[:, :size]
    work[...] = matrix[...]
    inverse = factor_inverse(work, diag, panel)
    half = split_dot(inverse, summed_ref[:, size:], (1, 0), 3)
    root_coef = split_dot(inverse, half, (0, 0), 3)
    coef = solved_ref[:, size:] - split_dot(solved_ref[:, :size], root_coef, (1, 0), 3)
    knots = coef.shape[0]
    pick = one_hot(knot_ref[:, :knots], pool.shape[1])
    spread = jnp.dot(pick, coef.astype(BF16), preferred_element_type=F32).astype(BF16)
    factor_ref[...] = factor_rows(matrix, first, inverse, scale)
    for load in loads:
        load.wait()
    mean = jnp.dot(pool[...], spread, preferred_element_type=F32)
    mean = mean + jnp.dot(root[...], root_coef.astype(BF16), preferred_element_type=F32)
    pred_ref[0] = mean.astype(BF16)


VMEM = pl.BlockSpec(memory_space=pltpu.VMEM)
SMEM = pl.BlockSpec(memory_space=pltpu.SMEM)
ANY = pl.BlockSpec(memory_space=pl.ANY)


def per_device(
    leaf_factor, basis_pool, root_basis, responses, knot_order, region_prior, root_prior
):
    knots = region_prior.shape[1]
    roots = root_prior.shape[0]
    cols = responses.shape[2]
    leaf_count = lax.axis_size("leaf")
    region_count = lax.axis_size("region")
    chips = leaf_count // 2
    rows = leaf_factor.shape[2]
    pool = basis_pool.shape[2]
    leaf = lax.axis_index("leaf").astype(jnp.int32)
    leaf_at = leaf.reshape(1)
    core_at = lax.rem(leaf, 2).reshape(1)
    share = knots // leaf_count
    wide_b = knots + roots + cols
    wide_a = roots + cols

    def shape(*dims):
        return jax.ShapeDtypeStruct(dims, F32)

    piece = shape(chips, share, wide_b + wide_a)
    keep, send = pl.pallas_call(
        grams_kernel,
        out_shape=(piece, piece),
        in_specs=[SMEM, VMEM, ANY, ANY, ANY, ANY],
        out_specs=(VMEM, VMEM),
        scratch_shapes=[
            pltpu.VMEM((rows, wide_b), BF16),
            pltpu.VMEM((rows, rows), BF16),
            pltpu.VMEM((rows, pool), BF16),
            pltpu.VMEM((2, chips, share, wide_b + wide_a), F32),
            pltpu.SemaphoreType.DMA((4,)),
        ],
        name="grams",
    )(core_at, knot_order, leaf_factor, basis_pool, root_basis, responses)

    swap = [(i, i ^ 1) for i in range(leaf_count)]
    same_core = [list(range(c, leaf_count, 2)) for c in range(2)]
    same_chip = [[i, i + 1] for i in range(0, leaf_count, 2)]
    paired = keep + lax.ppermute(send, "leaf", swap)
    arrived = lax.all_to_all(paired, "leaf", 0, 0, axis_index_groups=same_core, tiled=True)
    column = lax.all_gather(
        arrived.sum(axis=0), "leaf", axis=0, axis_index_groups=same_core, tiled=True
    )
    gathered = lax.all_gather(
        column[:, :wide_b], "leaf", axis=0, axis_index_groups=same_chip, tiled=True
    )

    square = pltpu.VMEM((knots, knots), F32)
    small = [pltpu.VMEM((STEP, 128), F32), pltpu.VMEM((STEP * knots // 128, 128), F32)]
    obs = rows * leaf_count
    chunk = roots // region_count // 2
    part = shape(region_count, chunk, wide_a)
    solved, schur, region_factor = pl.pallas_call(
        lambda *refs: region_kernel(1.0 / math.sqrt(obs), *refs),
        out_shape=(shape(knots, wide_a), part, shape(1, share, knots)),
        in_specs=[SMEM, VMEM, VMEM, VMEM],
        out_specs=(VMEM,) * 3,
        scratch_shapes=[square, square, *small, pltpu.VMEM((knots, wide_a), F32)],
        name="region_solve",
    )(leaf_at, gathered, column, region_prior)

    schur = lax.all_to_all(schur, "region", 0, 0, tiled=True)
    copies = jnp.broadcast_to(schur.sum(axis=0)[None], part.shape)
    summed = lax.all_to_all(copies, "region", 0, 0, tiled=True).reshape(roots // 2, wide_a)
    summed = lax.all_gather(summed, "leaf", axis=0, axis_index_groups=same_chip, tiled=True)

    predictions, root_factor = pl.pallas_call(
        lambda *refs: root_kernel(1.0 / math.sqrt(obs * region_count), *refs),
        out_shape=(
            jax.ShapeDtypeStruct((1, rows, cols), BF16),
            jax.ShapeDtypeStruct((share, roots), F32),
        ),
        in_specs=[SMEM, VMEM, VMEM, VMEM, VMEM, ANY, ANY],
        out_specs=(VMEM, VMEM),
        scratch_shapes=[
            square, square, *small,
            pltpu.VMEM((rows, pool), BF16),
            pltpu.VMEM((rows, roots), BF16),
            pltpu.SemaphoreType.DMA((2,)),
        ],
        name="root_solve",
    )(leaf_at, summed, root_prior, solved, knot_order, basis_pool, root_basis)
    return predictions, region_factor, root_factor


def solution(mesh):
    placed = (
        P("region", "leaf", None),
        P("region", "leaf", None),
        P("region", "leaf", None),
        P("region", "leaf", None),
        P("region", None),
        P("region", None, None),
        P(),
    )
    return jax.shard_map(
        per_device,
        mesh=mesh,
        in_specs=placed,
        out_specs=(P("region", "leaf", None), P("region", "leaf", None), P("leaf", None)),
        check_vma=False,
    )
```

time: 182 us -> 161 us (0.88)
  blocking collectives: 127 us -> 111 us
  Pallas kernels: 40.5 us -> 37.7 us
    all_gather x2 -> x3, blocking collectives: 69 us -> 41.7 us  [the longest x1 26.3 us: per_device(): lax.all_gather(arrived.sum(axis=0), 'leaf', axis=0, axis_index_groups=sam...]
    all_to_all x1 -> x2, blocking collectives: 14.3 us -> 25.2 us  [the longest x1 14.3 us: per_device(): schur = lax.all_to_all(schur, 'region', 0, 0, tiled=True)]
where the time goes in v4:
time: 161 us
  blocking collectives  111 us (69%)
  Pallas kernels  37.7 us (23%)
  starting transfers between devices  8.75 us (5%)
  waiting for transfers between devices  1.91 us (1%)
    all_to_all x1, blocking collectives, per_device(): lax.all_to_all(paired, 'leaf', 0, 0, axis_index_groups=same_core, tiled=T...  43.8 us
    all_gather x1, blocking collectives, per_device(): lax.all_gather(arrived.sum(axis=0), 'leaf', axis=0, axis_index_groups=sam...  26.3 us
    pallas_call x1, Pallas kernels, per_device(): pl.pallas_call(lambda *refs: root_kernel(1.0 / math.sqrt(obs * region_cou...  15.7 us
    pallas_call x1, Pallas kernels, per_device(): pl.pallas_call(lambda *refs: region_kernel(1.0 / math.sqrt(obs), *refs),...  15.1 us
    all_to_all x1, blocking collectives, per_device(): schur = lax.all_to_all(schur, 'region', 0, 0, tiled=True)  14.3 us
    all_to_all x1, blocking collectives, per_device(): lax.all_to_all(copies, 'region', 0, 0, tiled=True)  10.8 us
    all_gather x1, blocking collectives, per_device(): lax.all_gather(column[:, :wide_b], 'leaf', axis=0, axis_index_groups=same...  10.5 us
    ppermute x1, starting transfers between devices, per_device(): paired = keep + lax.ppermute(send, 'leaf', swap)  8.75 us
  transfers between devices with their start and end apart: 1, of which 1 were waited for; matrix products, arithmetic and copies ran while one was open for 0% of the time, Pallas kernels for 0%

profile of v4, /device:TPU:1, one launch (start us, length us, event | category | flops | bytes accessed | tf_op | source)
XLA Modules:
  0.0 160.9 jit_solution(12619433445019821770)
XLA Ops:
  0.6 6.9 %grams.1 = (f32[16,8,1280]{2,1,0:T(8,128)}, f32[16,8,1280]{2,1,0:T(8,128)}) custom-call(s32[1]{0:T(128)} %bitcast.1.core_ref, s32[1,512]{1,0:T(1,128)} %refs_4_.1, bf16[1,1024,1024]{2,1,0:T(8,128)(2,1)} %factor_hbm.1, bf16[1,1024,512]{2,1,0:T(8,128)(2,1)} %refs_5_.1, bf16[1,1024,256]{2,1,0:T(8,128)(2,1)} %refs_6_.1, bf16[1,1024,256]{2,1,0:T(8,128)(2,1)} %resp_hbm.1), custom_call_target="tpu_custom_call" | custom-call | tf_op jit(solution)/shard_map/grams/pallas_call | solution.py:215
  7.5 8.7 %collective-permute-start = (f32[16,8,1280]{2,1,0:T(8,128)}, f32[16,8,1280]{2,1,0:T(8,128)S(1)}, u32[]{:S(2)}, u32[]{:S(2)}) collective-permute-start(f32[16,8,1280]{2,1,0:T(8,128)} %get-tuple-element.11), channel_id=1, source_target_pairs={{0,16},{16,0},{32,48},{48,32},{64,80},{80,64},{96,112},{112,96},{1... | collective-permute-start | bytes 1966088 | tf_op jit(solution)/shard_map/ppermute | solution.py:233
  16.3 1.9 %collective-permute-done = f32[16,8,1280]{2,1,0:T(8,128)S(1)} collective-permute-done((f32[16,8,1280]{2,1,0:T(8,128)}, f32[16,8,1280]{2,1,0:T(8,128)S(1)}, u32[]{:S(2)}, u32[]{:S(2)}) %collective-permute-start) | collective-permute-done | bytes 655392 | tf_op jit(solution)/shard_map/ppermute | solution.py:233
  18.2 1.2 add.3
  19.3 43.8 %all_to_all.15 = f32[16,8,1280]{2,1,0:T(8,128)S(1)} all-to-all(f32[16,8,1280]{2,1,0:T(8,128)S(1)} %add.3), channel_id=1, replica_groups={{0,32,64,96,128,160,192,224,256,288,320,352,384,416,448,480},{16,48,80,..., dimensions={0} | all-to-all | bytes 1310720 | tf_op jit(solution)/shard_map/all_to_all | solution.py:234
  63.2 26.3 %all_gather.9.refs_2_ = f32[128,1280]{1,0:T(8,128)S(1)} all-gather(f32[8,1280]{1,0:T(8,128)S(1)} %reduce_sum.18), channel_id=1, replica_groups={{0,32,64,96,128,160,192,224,256,288,320,352,384,416,448,480},{16,48,80,..., dimensions={0}, use_global_device_ids=true | all-gather | bytes 696320 | tf_op jit(solution)/shard_map/all_gather | solution.py:235
  89.5 0.0 copy-start
  89.5 10.5 %all_gather.10.refs_1_ = f32[256,768]{1,0:T(8,128)} all-gather(f32[128,768]{1,0:T(8,128)S(1)} %slice.4), channel_id=1, replica_groups={{0,16},{32,48},{64,80},{96,112},{128,144},{160,176},{192,208},{224,240}..., dimensions={0}, use_global_device_ids=true | all-gather | bytes 1179648 | tf_op jit(solution)/shard_map/all_gather | solution.py:238
  100.0 0.0 copy-done
  100.0 15.1 %region_solve.1 = (f32[256,512]{1,0:T(8,128)}, f32[16,8,512]{2,1,0:T(8,128)}, f32[1,8,256]{2,1,0:T(8,128)}) custom-call(s32[1]{0:T(128)} %bitcast.refs_0_, f32[256,768]{1,0:T(8,128)} %all_gather.10.refs_1_, f32[128,1280]{1,0:T(8,128)} %copy-done, bf16[1,256,256]{2,1,0:T(8,128)(2,1)} %refs_3_.1), custom_call_target="tpu_custom_call" | custom-call | tf_op jit(solution)/shard_map/region_solve/pallas_call | solution.py:247
  115.1 14.3 %all_to_all.16 = f32[16,8,512]{2,1,0:T(8,128)S(1)} all-to-all(f32[16,8,512]{2,1,0:T(8,128)} %get-tuple-element.12), channel_id=1, replica_groups=mesh['leaf'=32,'region'=16] {'region'}, dimensions={0} | all-to-all | bytes 524288 | tf_op jit(solution)/shard_map/all_to_all | solution.py:256
  129.5 10.8 %all_to_all.17 = f32[16,8,512]{2,1,0:T(8,128)S(1)} all-to-all(f32[16,8,512]{2,1,0:T(8,128)S(1)} %broadcast_in_dim.2), channel_id=1, replica_groups=mesh['leaf'=32,'region'=16] {'region'}, dimensions={0} | all-to-all | bytes 524288 | tf_op jit(solution)/shard_map/all_to_all | solution.py:258
  140.3 4.9 %all_gather.11.refs_1_ = f32[256,512]{1,0:T(8,128)} all-gather(f32[128,512]{1,0:T(8,128)S(1)} %bitcast.3), channel_id=1, replica_groups={{0,16},{32,48},{64,80},{96,112},{128,144},{160,176},{192,208},{224,240}..., dimensions={0}, use_global_device_ids=true | all-gather | bytes 786432 | tf_op jit(solution)/shard_map/all_gather | solution.py:259
  145.2 15.7 %root_solve.1 = (bf16[1,1024,256]{2,1,0:T(8,128)(2,1)}, f32[8,256]{1,0:T(8,128)}) custom-call(s32[1]{0:T(128)} %bitcast.refs_0_, f32[256,512]{1,0:T(8,128)} %all_gather.11.refs_1_, bf16[256,256]{1,0:T(8,128)(2,1)} %refs_2_.1, f32[256,512]{1,0:T(8,128)} %get-tuple-element.13.refs_3_, s32[1,512]{1,0:T(1,128)} %refs_4_.1, bf16[1,1024,512]{2,1,0:T(8,128)(2,1)} %refs_5_.1, ...), custom_call_target="tpu_custom_call" | custom-call | tf_op jit(solution)/shard_map/root_solve/pallas_call | solution.py:261
  (4 shorter events, 0.1 us)
Async XLA Ops:
  7.5 10.7 %collective-permute-start = (f32[16,8,1280]{2,1,0:T(8,128)}, f32[16,8,1280]{2,1,0:T(8,128)S(1)}, u32[]{:S(2)}, u32[]{:S(2)}) collective-permute-start(f32[16,8,1280]{2,1,0:T(8,128)} %get-tuple-element.11), channel_id=1, source_target_pairs={{0,16},{16,0},{32,48},{48,32},{64,80},{80,64},{96,112},{112,96},{1... | collective-permute-start | bytes 1966088 | tf_op jit(solution)/shard_map/ppermute | solution.py:233
  89.5 10.6 %copy-start = (f32[128,1280]{1,0:T(8,128)}, f32[128,1280]{1,0:T(8,128)S(1)}, u32[]{:S(2)}) copy-start(f32[128,1280]{1,0:T(8,128)S(1)} %all_gather.9.refs_2_) | copy-start | bytes 1966084

commit v5 on v4

--- a/solution.py
+++ b/solution.py
@@ -1,3 +1,4 @@
+import functools
 import math
 
 import jax
@@ -49,8 +50,16 @@
     white = rows_dot(factor[...], joined[...]).astype(BF16)
     gram_b = rows_dot(white[:, :knots], white)
     gram_a = rows_dot(white[:, knots : knots + roots], white[:, knots:])
-    total[:, :, :, :width] = gram_b.reshape(*total.shape[:3], width)
-    total[:, :, :, width:] = gram_a.reshape(*total.shape[:3], gram_a.shape[1])
+    rows = knots // 2
+    for side in range(2):
+        mine = slice(side * rows, (side + 1) * rows)
+        cross = gram_a[mine, rows:roots] if side == 0 else gram_b[mine, :rows]
+        parts = (gram_b[mine, mine], cross, gram_b[mine, knots:], gram_a[mine, mine], gram_a[mine, roots:])
+        at = 0
+        for part in parts:
+            wide = part.shape[1]
+            total[side, :, :, at : at + wide] = part.reshape(*total.shape[1:3], wide)
+            at += wide
     core = core_ref[0]
     keep_ref[...] = total[core]
     send_ref[...] = total[1 - core]
@@ -78,11 +87,10 @@
     size = work.shape[0]
     tiles = size // 128
 
-    def block(k, _):
+    def block(base, k, _):
         start = pl.multiple_of(k * STEP, STEP)
-        tile = pl.multiple_of((start // 128) * 128, 128)
-        corner = work[pl.ds(start, STEP), pl.ds(tile, 128)]
-        diag[...] = pltpu.roll(corner, lax.rem(128 - (start - tile), 128), 1)
+        corner = work[pl.ds(start, STEP), base : base + 128]
+        diag[...] = pltpu.roll(corner, lax.rem(128 - (start - base), 128), 1)
         held = work[pl.ds(start, STEP), :]
         sub = lax.broadcasted_iota(jnp.int32, (8, 128), 0)
         at = sub * 128 + lax.broadcasted_iota(jnp.int32, (8, 128), 1) - start
@@ -115,15 +123,16 @@
         th, tm, tl = (jnp.where(later, x, zero) for x in (high, mid, low))
         left = jnp.concatenate([th, th, tm, th, tl, tm], axis=0)
         right = jnp.concatenate([high, mid, high, low, high, mid], axis=0)
-        change = rows_dot(left, right)
-        lane_a = lax.broadcasted_iota(jnp.int32, (size, size), 1)
-        row_a = lax.broadcasted_iota(jnp.int32, (size, size), 0)
+        change = rows_dot(left[:, base:], right)
+        lane_a = lax.broadcasted_iota(jnp.int32, change.shape, 1)
+        row_a = lax.broadcasted_iota(jnp.int32, change.shape, 0) + base
         fresh = (lane_a >= start) & (lane_a < start + STEP) & (row_a >= start + STEP)
-        work[...] = jnp.where(fresh, 0.0, work[...]) - change
+        work[base:, :] = jnp.where(fresh, 0.0, work[base:, :]) - change
         work[pl.ds(start, STEP), :] = rows
         return 0
 
-    lax.fori_loop(0, size // STEP, block, 0)
+    for base in range(0, size, 128):
+        lax.fori_loop(base // STEP, (base + 128) // STEP, functools.partial(block, base), 0)
     lane = lax.broadcasted_iota(jnp.int32, (size, size), 1)
     row = lax.broadcasted_iota(jnp.int32, (size, size), 0)
     return jnp.where(lane <= row, work[...], 0.0)
@@ -144,15 +153,30 @@
     first = leaf_ref[0] * 8
     width = size + solved_ref.shape[1]
     count = schur_ref.shape[0] * schur_ref.shape[1]
-    mine = pl.multiple_of(lax.rem(leaf_ref[0], 2) * count, count)
-    matrix[...] = prior_ref[0].astype(F32) + gathered_ref[:, :size]
+    core = lax.rem(leaf_ref[0], 2)
+    mine = pl.multiple_of(core * count, count)
+    lower = gathered_ref[count:, count:size]
+    matrix[:count, :count] = gathered_ref[:count, :count]
+    matrix[count:, count:] = gathered_ref[count:, :count]
+    matrix[count:, :count] = lower
+    matrix[:count, count:] = lower.T
+    matrix[...] += prior_ref[0].astype(F32)
     work[...] = matrix[...]
     inverse = factor_inverse(work, diag, panel)
     half = split_dot(inverse, gathered_ref[:, size:width], (1, 0))
     half_ref[...] = half
-    schur = column_ref[:, width:] - split_dot(
-        half_ref[:, pl.ds(mine, count)], half, (0, 0)
-    )
+    upper = gathered_ref[:count, count:size]
+    near = column_ref[:, width : width + count]
+    cross = jnp.where(core == 0, upper, upper.T)
+    own = jnp.concatenate(
+        [
+            jnp.where(core == 0, near, cross),
+            jnp.where(core == 0, cross, near),
+            column_ref[:, width + count :],
+        ],
+        axis=1,
+    )
+    schur = own - split_dot(half_ref[:, pl.ds(mine, count)], half, (0, 0))
     schur_ref[...] = schur.reshape(schur_ref.shape)
     solved_ref[...] = split_dot(inverse, half, (0, 0), 3)
     factor_ref[0] = factor_rows(matrix, first, inverse, scale)
@@ -211,7 +235,8 @@
     def shape(*dims):
         return jax.ShapeDtypeStruct(dims, F32)
 
-    piece = shape(chips, share, wide_b + wide_a)
+    width = wide_b + wide_a - knots // 2
+    piece = shape(chips, share, width)
     keep, send = pl.pallas_call(
         grams_kernel,
         out_shape=(piece, piece),
@@ -221,7 +246,7 @@
             pltpu.VMEM((rows, wide_b), BF16),
             pltpu.VMEM((rows, rows), BF16),
             pltpu.VMEM((rows, pool), BF16),
-            pltpu.VMEM((2, chips, share, wide_b + wide_a), F32),
+            pltpu.VMEM((2, chips, share, width), F32),
             pltpu.SemaphoreType.DMA((4,)),
         ],
         name="grams",

time: 161 us -> 158 us (0.981)
  blocking collectives: 111 us -> 108 us
    all_gather x1, blocking collectives: 26.3 us -> 24.2 us  [per_device(): lax.all_gather(arrived.sum(axis=0), 'leaf', axis=0, axis_index_groups=sam...]
where the time goes in v5:
time: 158 us
  blocking collectives  108 us (68%)
  Pallas kernels  37.3 us (24%)
  starting transfers between devices  8.75 us (6%)
  waiting for transfers between devices  1.82 us (1%)
    all_to_all x1, blocking collectives, per_device(): lax.all_to_all(paired, 'leaf', 0, 0, axis_index_groups=same_core, tiled=T...  43 us
    all_gather x1, blocking collectives, per_device(): lax.all_gather(arrived.sum(axis=0), 'leaf', axis=0, axis_index_groups=sam...  24.2 us
    pallas_call x1, Pallas kernels, per_device(): pl.pallas_call(lambda *refs: root_kernel(1.0 / math.sqrt(obs * region_cou...  15.6 us
    pallas_call x1, Pallas kernels, per_device(): pl.pallas_call(lambda *refs: region_kernel(1.0 / math.sqrt(obs), *refs),...  14.9 us
    all_to_all x1, blocking collectives, per_device(): schur = lax.all_to_all(schur, 'region', 0, 0, tiled=True)  14.3 us
    all_to_all x1, blocking collectives, per_device(): lax.all_to_all(copies, 'region', 0, 0, tiled=True)  10.8 us
    all_gather x1, blocking collectives, per_device(): lax.all_gather(column[:, :wide_b], 'leaf', axis=0, axis_index_groups=same...  10.8 us
    ppermute x1, starting transfers between devices, per_device(): paired = keep + lax.ppermute(send, 'leaf', swap)  8.75 us
  transfers between devices with their start and end apart: 1, of which 1 were waited for; matrix products, arithmetic and copies ran while one was open for 0% of the time, Pallas kernels for 0%

profile of v5, /device:TPU:1, one launch (start us, length us, event | category | flops | bytes accessed | tf_op | source)
XLA Modules:
  0.0 157.9 jit_solution(12974321002124019978)
XLA Ops:
  0.6 6.8 %grams.1 = (f32[16,8,1152]{2,1,0:T(8,128)}, f32[16,8,1152]{2,1,0:T(8,128)}) custom-call(s32[1]{0:T(128)} %bitcast.1.core_ref, s32[1,512]{1,0:T(1,128)} %refs_4_.1, bf16[1,1024,1024]{2,1,0:T(8,128)(2,1)} %factor_hbm.1, bf16[1,1024,512]{2,1,0:T(8,128)(2,1)} %refs_5_.1, bf16[1,1024,256]{2,1,0:T(8,128)(2,1)} %refs_6_.1, bf16[1,1024,256]{2,1,0:T(8,128)(2,1)} %resp_hbm.1), custom_call_target="tpu_custom_call" | custom-call | tf_op jit(solution)/shard_map/grams/pallas_call | solution.py:240
  7.5 8.7 %collective-permute-start = (f32[16,8,1152]{2,1,0:T(8,128)}, f32[16,8,1152]{2,1,0:T(8,128)S(1)}, u32[]{:S(2)}, u32[]{:S(2)}) collective-permute-start(f32[16,8,1152]{2,1,0:T(8,128)} %get-tuple-element.11), channel_id=1, source_target_pairs={{0,16},{16,0},{32,48},{48,32},{64,80},{80,64},{96,112},{112,96},{1... | collective-permute-start | bytes 1769480 | tf_op jit(solution)/shard_map/ppermute | solution.py:258
  16.2 1.8 %collective-permute-done = f32[16,8,1152]{2,1,0:T(8,128)S(1)} collective-permute-done((f32[16,8,1152]{2,1,0:T(8,128)}, f32[16,8,1152]{2,1,0:T(8,128)S(1)}, u32[]{:S(2)}, u32[]{:S(2)}) %collective-permute-start) | collective-permute-done | bytes 589856 | tf_op jit(solution)/shard_map/ppermute | solution.py:258
  18.0 1.1 add.3
  19.2 43.0 %all_to_all.15 = f32[16,8,1152]{2,1,0:T(8,128)S(1)} all-to-all(f32[16,8,1152]{2,1,0:T(8,128)S(1)} %add.3), channel_id=1, replica_groups={{0,32,64,96,128,160,192,224,256,288,320,352,384,416,448,480},{16,48,80,..., dimensions={0} | all-to-all | bytes 1179648 | tf_op jit(solution)/shard_map/all_to_all | solution.py:259
  62.2 24.2 %all_gather.9.refs_2_ = f32[128,1152]{1,0:T(8,128)S(1)} all-gather(f32[8,1152]{1,0:T(8,128)S(1)} %reduce_sum.18), channel_id=1, replica_groups={{0,32,64,96,128,160,192,224,256,288,320,352,384,416,448,480},{16,48,80,..., dimensions={0}, use_global_device_ids=true | all-gather | bytes 626688 | tf_op jit(solution)/shard_map/all_gather | solution.py:260
  86.5 0.0 copy-start
  86.5 10.8 %all_gather.10.refs_1_ = f32[256,768]{1,0:T(8,128)} all-gather(f32[128,768]{1,0:T(8,128)S(1)} %slice.4), channel_id=1, replica_groups={{0,16},{32,48},{64,80},{96,112},{128,144},{160,176},{192,208},{224,240}..., dimensions={0}, use_global_device_ids=true | all-gather | bytes 1179648 | tf_op jit(solution)/shard_map/all_gather | solution.py:263
  97.3 0.0 copy-done
  97.3 14.9 %region_solve.1 = (f32[256,512]{1,0:T(8,128)}, f32[16,8,512]{2,1,0:T(8,128)}, f32[1,8,256]{2,1,0:T(8,128)}) custom-call(s32[1]{0:T(128)} %bitcast.refs_0_, f32[256,768]{1,0:T(8,128)} %all_gather.10.refs_1_, f32[128,1152]{1,0:T(8,128)} %copy-done, bf16[1,256,256]{2,1,0:T(8,128)(2,1)} %refs_3_.1), custom_call_target="tpu_custom_call" | custom-call | tf_op jit(solution)/shard_map/region_solve/pallas_call | solution.py:272
  112.2 14.3 %all_to_all.16 = f32[16,8,512]{2,1,0:T(8,128)S(1)} all-to-all(f32[16,8,512]{2,1,0:T(8,128)} %get-tuple-element.12), channel_id=1, replica_groups=mesh['leaf'=32,'region'=16] {'region'}, dimensions={0} | all-to-all | bytes 524288 | tf_op jit(solution)/shard_map/all_to_all | solution.py:281
  126.6 10.8 %all_to_all.17 = f32[16,8,512]{2,1,0:T(8,128)S(1)} all-to-all(f32[16,8,512]{2,1,0:T(8,128)S(1)} %broadcast_in_dim.2), channel_id=1, replica_groups=mesh['leaf'=32,'region'=16] {'region'}, dimensions={0} | all-to-all | bytes 524288 | tf_op jit(solution)/shard_map/all_to_all | solution.py:283
  137.4 4.9 %all_gather.11.refs_1_ = f32[256,512]{1,0:T(8,128)} all-gather(f32[128,512]{1,0:T(8,128)S(1)} %bitcast.3), channel_id=1, replica_groups={{0,16},{32,48},{64,80},{96,112},{128,144},{160,176},{192,208},{224,240}..., dimensions={0}, use_global_device_ids=true | all-gather | bytes 786432 | tf_op jit(solution)/shard_map/all_gather | solution.py:284
  142.3 15.6 %root_solve.1 = (bf16[1,1024,256]{2,1,0:T(8,128)(2,1)}, f32[8,256]{1,0:T(8,128)}) custom-call(s32[1]{0:T(128)} %bitcast.refs_0_, f32[256,512]{1,0:T(8,128)} %all_gather.11.refs_1_, bf16[256,256]{1,0:T(8,128)(2,1)} %refs_2_.1, f32[256,512]{1,0:T(8,128)} %get-tuple-element.13.refs_3_, s32[1,512]{1,0:T(1,128)} %refs_4_.1, bf16[1,1024,512]{2,1,0:T(8,128)(2,1)} %refs_5_.1, ...), custom_call_target="tpu_custom_call" | custom-call | tf_op jit(solution)/shard_map/root_solve/pallas_call | solution.py:286
  (4 shorter events, 0.1 us)
Async XLA Ops:
  7.5 10.6 %collective-permute-start = (f32[16,8,1152]{2,1,0:T(8,128)}, f32[16,8,1152]{2,1,0:T(8,128)S(1)}, u32[]{:S(2)}, u32[]{:S(2)}) collective-permute-start(f32[16,8,1152]{2,1,0:T(8,128)} %get-tuple-element.11), channel_id=1, source_target_pairs={{0,16},{16,0},{32,48},{48,32},{64,80},{80,64},{96,112},{112,96},{1... | collective-permute-start | bytes 1769480 | tf_op jit(solution)/shard_map/ppermute | solution.py:258
  86.5 10.8 %copy-start = (f32[128,1152]{1,0:T(8,128)}, f32[128,1152]{1,0:T(8,128)S(1)}, u32[]{:S(2)}) copy-start(f32[128,1152]{1,0:T(8,128)S(1)} %all_gather.9.refs_2_) | copy-start | bytes 1769476

commit v6 on v5

--- a/solution.py
+++ b/solution.py
@@ -26,8 +26,8 @@
     return (ids == knots).astype(BF16)
 
 
-def grams_kernel(core_ref, knot_ref, factor_hbm, pool_hbm, root_hbm, resp_hbm,
-                 keep_ref, send_ref, joined, factor, pool, total, sems):
+def grams_kernel(knot_ref, factor_hbm, pool_hbm, root_hbm, resp_hbm,
+                 total, joined, factor, pool, sems):
     roots = root_hbm.shape[2]
     width = joined.shape[1]
     knots = width - roots - resp_hbm.shape[2]
@@ -60,9 +60,6 @@
             wide = part.shape[1]
             total[side, :, :, at : at + wide] = part.reshape(*total.shape[1:3], wide)
             at += wide
-    core = core_ref[0]
-    keep_ref[...] = total[core]
-    send_ref[...] = total[1 - core]
 
 
 def split3(x):
@@ -227,7 +224,6 @@
     pool = basis_pool.shape[2]
     leaf = lax.axis_index("leaf").astype(jnp.int32)
     leaf_at = leaf.reshape(1)
-    core_at = lax.rem(leaf, 2).reshape(1)
     share = knots // leaf_count
     wide_b = knots + roots + cols
     wide_a = roots + cols
@@ -236,26 +232,24 @@
         return jax.ShapeDtypeStruct(dims, F32)
 
     width = wide_b + wide_a - knots // 2
-    piece = shape(chips, share, width)
-    keep, send = pl.pallas_call(
+    halves = pl.pallas_call(
         grams_kernel,
-        out_shape=(piece, piece),
-        in_specs=[SMEM, VMEM, ANY, ANY, ANY, ANY],
-        out_specs=(VMEM, VMEM),
+        out_shape=shape(2, chips, share, width),
+        in_specs=[VMEM, ANY, ANY, ANY, ANY],
+        out_specs=VMEM,
         scratch_shapes=[
             pltpu.VMEM((rows, wide_b), BF16),
             pltpu.VMEM((rows, rows), BF16),
             pltpu.VMEM((rows, pool), BF16),
-            pltpu.VMEM((2, chips, share, width), F32),
             pltpu.SemaphoreType.DMA((4,)),
         ],
         name="grams",
-    )(core_at, knot_order, leaf_factor, basis_pool, root_basis, responses)
-
-    swap = [(i, i ^ 1) for i in range(leaf_count)]
+    )(knot_order, leaf_factor, basis_pool, root_basis, responses)
+
     same_core = [list(range(c, leaf_count, 2)) for c in range(2)]
     same_chip = [[i, i + 1] for i in range(0, leaf_count, 2)]
-    paired = keep + lax.ppermute(send, "leaf", swap)
+    paired = lax.all_to_all(halves, "leaf", 0, 0, axis_index_groups=same_chip, tiled=True)
+    paired = paired.sum(axis=0)
     arrived = lax.all_to_all(paired, "leaf", 0, 0, axis_index_groups=same_core, tiled=True)
     column = lax.all_gather(
         arrived.sum(axis=0), "leaf", axis=0, axis_index_groups=same_core, tiled=True

time: 158 us -> 161 us (1.019)
  waiting for transfers between devices: 1.82 us -> 25.3 us
  blocking collectives: 108 us -> 86.1 us
    all_to_all x1, blocking collectives: 43 us -> 12.3 us  [per_device(): lax.all_to_all(halves, 'leaf', 0, 0, axis_index_groups=same_chip, tiled=T...]
    all_to_all x0 -> x1, waiting for transfers between devices: none -> 25.3 us  [per_device(): lax.all_to_all(paired, 'leaf', 0, 0, axis_index_groups=same_core, tiled=T...]
    all_to_all x0 -> x1, starting transfers between devices: none -> 9.57 us  [per_device(): lax.all_to_all(paired, 'leaf', 0, 0, axis_index_groups=same_core, tiled=T...]
    ppermute x1 -> x0, starting transfers between devices: 8.75 us -> none  [per_device(): paired = keep + lax.ppermute(send, 'leaf', swap)]
    all_gather x1, blocking collectives: 24.2 us -> 29.5 us  [per_device(): lax.all_gather(arrived.sum(axis=0), 'leaf', axis=0, axis_index_groups=sam...]
    all_gather x1, blocking collectives: 10.8 us -> 14.3 us  [per_device(): lax.all_gather(column[:, :wide_b], 'leaf', axis=0, axis_index_groups=same...]
    ppermute x1 -> x0, waiting for transfers between devices: 1.82 us -> none  [per_device(): paired = keep + lax.ppermute(send, 'leaf', swap)]
where the time goes in v6:
time: 161 us; the launch traced here: 160 us
  blocking collectives  86.1 us (53%)
  Pallas kernels  37.3 us (23%)
  waiting for transfers between devices  25.3 us (16%)
  starting transfers between devices  9.57 us (6%)
    all_gather x1, blocking collectives, per_device(): lax.all_gather(arrived.sum(axis=0), 'leaf', axis=0, axis_index_groups=sam...  29.5 us
    all_to_all x1, waiting for transfers between devices, per_device(): lax.all_to_all(paired, 'leaf', 0, 0, axis_index_groups=same_core, tiled=T...  25.3 us
    pallas_call x1, Pallas kernels, per_device(): pl.pallas_call(lambda *refs: root_kernel(1.0 / math.sqrt(obs * region_cou...  15.6 us
    pallas_call x1, Pallas kernels, per_device(): pl.pallas_call(lambda *refs: region_kernel(1.0 / math.sqrt(obs), *refs),...  14.9 us
    all_gather x1, blocking collectives, per_device(): lax.all_gather(column[:, :wide_b], 'leaf', axis=0, axis_index_groups=same...  14.3 us
    all_to_all x1, blocking collectives, per_device(): schur = lax.all_to_all(schur, 'region', 0, 0, tiled=True)  14.3 us
    all_to_all x1, blocking collectives, per_device(): lax.all_to_all(halves, 'leaf', 0, 0, axis_index_groups=same_chip, tiled=T...  12.3 us
    all_to_all x1, blocking collectives, per_device(): lax.all_to_all(copies, 'region', 0, 0, tiled=True)  10.8 us
  transfers between devices with their start and end apart: 1, of which 1 were waited for; matrix products, arithmetic and copies ran while one was open for 0% of the time, Pallas kernels for 0%

profile of v6, /device:TPU:1, one launch (start us, length us, event | category | flops | bytes accessed | tf_op | source)
XLA Modules:
  0.0 160.0 jit_solution(8081655459109339841)
XLA Ops:
  0.6 6.8 %grams.1 = f32[2,16,8,1152]{3,2,1,0:T(8,128)} custom-call(s32[1,512]{1,0:T(1,128)} %refs_4_.1, bf16[1,1024,1024]{2,1,0:T(8,128)(2,1)} %factor_hbm.1, bf16[1,1024,512]{2,1,0:T(8,128)(2,1)} %refs_5_.1, bf16[1,1024,256]{2,1,0:T(8,128)(2,1)} %refs_6_.1, bf16[1,1024,256]{2,1,0:T(8,128)(2,1)} %resp_hbm.1), custom_call_target="tpu_custom_call" | custom-call | tf_op jit(solution)/shard_map/grams/pallas_call | solution.py:235
  7.4 12.3 %all_to_all.20 = f32[2,16,8,1152]{3,2,1,0:T(8,128)S(1)} all-to-all(f32[2,16,8,1152]{3,2,1,0:T(8,128)} %grams.1), channel_id=1, replica_groups={{0,16},{32,48},{64,80},{96,112},{128,144},{160,176},{192,208},{224,240}..., dimensions={0} | all-to-all | bytes 2359296 | tf_op jit(solution)/shard_map/all_to_all | solution.py:251
  19.7 0.9 reduce_sum.27
  20.6 9.6 %all-to-all-start.1 = ((f32[16,8,1152]{2,1,0:T(8,128)}), f32[16,8,1152]{2,1,0:T(8,128)S(1)}, u32[]{:S(2)}, u32[]{:S(2)}) async-start(f32[16,8,1152]{2,1,0:T(8,128)} %reduce_sum.27), calls=%async_computation.1 | async-start | bytes 1179648 | tf_op jit(solution)/shard_map/all_to_all | solution.py:253
  30.2 25.3 %all-to-all-done.1 = f32[16,8,1152]{2,1,0:T(8,128)S(1)} async-done(((f32[16,8,1152]{2,1,0:T(8,128)}), f32[16,8,1152]{2,1,0:T(8,128)S(1)}, u32[]{:S(2)}, u32[]{:S(2)}) %all-to-all-start.1) | async-done | bytes 589856 | tf_op jit(solution)/shard_map/all_to_all | solution.py:253
  55.5 29.5 %all_gather.9.refs_2_ = f32[128,1152]{1,0:T(8,128)S(1)} all-gather(f32[8,1152]{1,0:T(8,128)S(1)} %reduce_sum.28), channel_id=1, replica_groups={{0,32,64,96,128,160,192,224,256,288,320,352,384,416,448,480},{16,48,80,..., dimensions={0}, use_global_device_ids=true | all-gather | bytes 626688 | tf_op jit(solution)/shard_map/all_gather | solution.py:254
  85.0 0.0 copy-start
  85.1 14.3 %all_gather.10.refs_1_ = f32[256,768]{1,0:T(8,128)} all-gather(f32[128,768]{1,0:T(8,128)S(1)} %slice.4), channel_id=1, replica_groups={{0,16},{32,48},{64,80},{96,112},{128,144},{160,176},{192,208},{224,240}..., dimensions={0}, use_global_device_ids=true | all-gather | bytes 1179648 | tf_op jit(solution)/shard_map/all_gather | solution.py:257
  99.4 0.0 copy-done
  99.4 14.9 %region_solve.1 = (f32[256,512]{1,0:T(8,128)}, f32[16,8,512]{2,1,0:T(8,128)}, f32[1,8,256]{2,1,0:T(8,128)}) custom-call(s32[1]{0:T(128)} %bitcast.refs_0_, f32[256,768]{1,0:T(8,128)} %all_gather.10.refs_1_, f32[128,1152]{1,0:T(8,128)} %copy-done, bf16[1,256,256]{2,1,0:T(8,128)(2,1)} %refs_3_.1), custom_call_target="tpu_custom_call" | custom-call | tf_op jit(solution)/shard_map/region_solve/pallas_call | solution.py:266
  114.3 14.3 %all_to_all.21 = f32[16,8,512]{2,1,0:T(8,128)S(1)} all-to-all(f32[16,8,512]{2,1,0:T(8,128)} %get-tuple-element.8), channel_id=1, replica_groups=mesh['leaf'=32,'region'=16] {'region'}, dimensions={0} | all-to-all | bytes 524288 | tf_op jit(solution)/shard_map/all_to_all | solution.py:275
  128.7 10.8 %all_to_all.22 = f32[16,8,512]{2,1,0:T(8,128)S(1)} all-to-all(f32[16,8,512]{2,1,0:T(8,128)S(1)} %broadcast_in_dim.2), channel_id=1, replica_groups=mesh['leaf'=32,'region'=16] {'region'}, dimensions={0} | all-to-all | bytes 524288 | tf_op jit(solution)/shard_map/all_to_all | solution.py:277
  139.6 4.9 %all_gather.11.refs_1_ = f32[256,512]{1,0:T(8,128)} all-gather(f32[128,512]{1,0:T(8,128)S(1)} %bitcast.2), channel_id=1, replica_groups={{0,16},{32,48},{64,80},{96,112},{128,144},{160,176},{192,208},{224,240}..., dimensions={0}, use_global_device_ids=true | all-gather | bytes 786432 | tf_op jit(solution)/shard_map/all_gather | solution.py:278
  144.4 15.6 %root_solve.1 = (bf16[1,1024,256]{2,1,0:T(8,128)(2,1)}, f32[8,256]{1,0:T(8,128)}) custom-call(s32[1]{0:T(128)} %bitcast.refs_0_, f32[256,512]{1,0:T(8,128)} %all_gather.11.refs_1_, bf16[256,256]{1,0:T(8,128)(2,1)} %refs_2_.1, f32[256,512]{1,0:T(8,128)} %get-tuple-element.9.refs_3_, s32[1,512]{1,0:T(1,128)} %refs_4_.1, bf16[1,1024,512]{2,1,0:T(8,128)(2,1)} %refs_5_.1, ...), custom_call_target="tpu_custom_call" | custom-call | tf_op jit(solution)/shard_map/root_solve/pallas_call | solution.py:280
  (4 shorter events, 0.1 us)
Async XLA Ops:
  20.6 34.9 %all-to-all-start.1 = ((f32[16,8,1152]{2,1,0:T(8,128)}), f32[16,8,1152]{2,1,0:T(8,128)S(1)}, u32[]{:S(2)}, u32[]{:S(2)}) async-start(f32[16,8,1152]{2,1,0:T(8,128)} %reduce_sum.27), calls=%async_computation.1 | async-start | bytes 1179648 | tf_op jit(solution)/shard_map/all_to_all | solution.py:253
  85.0 14.4 %copy-start = (f32[128,1152]{1,0:T(8,128)}, f32[128,1152]{1,0:T(8,128)S(1)}, u32[]{:S(2)}) copy-start(f32[128,1152]{1,0:T(8,128)S(1)} %all_gather.9.refs_2_) | copy-start | bytes 1769476
